TPU v7x, 256 devices: a whole 4x4x8 slice. The times are simulated.
256 devices in a mesh: col: 16 (over y, z_lo, core), row: 16 (over x, z_hi).
Axes of the slice: x: 4, y: 4, z: 8 (z_hi: 4, z_lo: 2; z = z_hi * 2 + z_lo), core: 2. Of those that a mesh axis runs over, the one named last changes fastest.
Arguments:
- object_field: float32 [2, 4608, 4608], P(None, 'row', 'col'), may hold values from -6 to 6
- probe: float32 [2, 256, 256], replicated, may hold values from -5 to 5
- amplitudes: bfloat16 [16, 16, 8, 256, 256], P('row', 'col'), may hold values from 0 to 2
- offsets: int32 [16, 16, 8, 2], P('row', 'col'), may hold values from 0 to 128
- counts: int32 [16, 16], P('row', 'col'), may hold values from 1 to 8
Outputs:
- updated_object: float32 [2, 4608, 4608], P(None, 'row', 'col')
All inputs are finite; a program needn't handle non-finite values.
Results may differ from a plain program's by a relative error of at most 0.0027.
Values sent between devices are 32-bit elements; how exact they have to be, the bound alone decides.
A program may use at most 64 MiB of HBM per device.

v0:
```python
import math

import jax
import jax.numpy as jnp
from jax import lax
from jax.sharding import PartitionSpec as P

MARGIN = 48
PASSES = 2


step_size = 0.1
soft_floor = 0.01


def with_halo(value, sides, width):
    for axis, dim in sides:
        size, length = (lax.axis_size(axis), value.shape[dim])
        up = [(i, (i + 1) % size) for i in range(size - 1)]
        down = [(j, i) for i, j in up]
        last = lax.slice_in_dim(value, length - width, length, axis=dim)
        first = lax.slice_in_dim(value, 0, width, axis=dim)
        before = lax.ppermute(last, axis, up)
        after = lax.ppermute(first, axis, down)
        value = jnp.concatenate([before, value, after], axis=dim)
    return value


def passed_along(value, axis, steps):
    count = lax.axis_size(axis)
    first, last = (max(0, -steps), min(count, count - steps))
    return lax.ppermute(value, axis, [(source, source + steps) for source in range(first, last)])


def dft_table(direction, length):
    position = jnp.arange(length, dtype=jnp.int32)
    angles = (position[:, None] * position[None, :] % length).astype(jnp.float32) * (
        2.0 * math.pi / length
    )
    norm_scale = 1.0 / math.sqrt(length)
    real_part = jnp.cos(angles) * norm_scale
    imag_part = jnp.sin(angles) * (direction * norm_scale)
    return jnp.stack(
        [jnp.stack([real_part, -imag_part]), jnp.stack([imag_part, real_part])]
    ).astype(jnp.bfloat16)


def transform(waves, table):
    first = jnp.einsum("cdkn,pdnm->pckm", table, waves, preferred_element_type=jnp.float32).astype(
        jnp.bfloat16
    )
    return jnp.einsum("cdkn,pdmn->pcmk", table, first, preferred_element_type=jnp.float32)


def cut_patches(tile_field, offset_list, side):

    def cut_patch(offset):
        return lax.dynamic_slice(tile_field, (jnp.int32(0), offset[0], offset[1]), (2, side, side))

    return jax.vmap(cut_patch)(offset_list)


def position_terms(tile_field, probe, measured, offset_list, live_slots, forward, inverse):
    side = probe.shape[-1]
    patches = cut_patches(tile_field, offset_list, side)
    probe_real, probe_imag = (probe[0], probe[1])
    exit_wave = jnp.stack(
        [
            probe_real * patches[:, 0] - probe_imag * patches[:, 1],
            probe_real * patches[:, 1] + probe_imag * patches[:, 0],
        ],
        axis=1,
    ).astype(jnp.bfloat16)
    far_field = transform(exit_wave, forward)
    magnitude = jnp.sqrt(
        far_field[:, 0] * far_field[:, 0] + far_field[:, 1] * far_field[:, 1] + soft_floor
    )
    factor = (measured.astype(jnp.float32) / magnitude - 1.0) * live_slots[:, None, None]
    correction = (far_field * factor[:, None]).astype(jnp.bfloat16)
    back_wave = transform(correction, inverse)
    return jnp.stack(
        [
            probe_real * back_wave[:, 0] + probe_imag * back_wave[:, 1],
            probe_real * back_wave[:, 1] - probe_imag * back_wave[:, 0],
        ],
        axis=1,
    )


def add_patch(current, term, offset):
    start = (jnp.int32(0), offset[0], offset[1])
    existing = lax.dynamic_slice(current, start, term.shape)
    return lax.dynamic_update_slice(current, existing + term, start)


def tile_gradient(tile_field, probe, measured, offset_list, live_count):
    side = probe.shape[-1]
    forward = dft_table(-1.0, side)
    inverse = dft_table(1.0, side)
    zeros_tile = jnp.zeros(tile_field.shape, jnp.float32)
    live_slots = (jnp.arange(offset_list.shape[0], dtype=jnp.int32) < live_count).astype(
        jnp.float32
    )
    terms = position_terms(tile_field, probe, measured, offset_list, live_slots, forward, inverse)

    def add_slot(slot, current):
        return add_patch(current, terms[slot], offset_list[slot])

    return lax.fori_loop(0, offset_list.shape[0], add_slot, zeros_tile)


def object_rim(current):
    return with_halo(current, (("col", 2), ("row", 1)), MARGIN)


def fold_col_margins(gradient):
    low_rim = gradient[:, :, :MARGIN]
    high_rim = gradient[:, :, -MARGIN:]
    from_next = passed_along(low_rim, "col", -1)
    from_prev = passed_along(high_rim, "col", 1)
    inner = gradient[:, :, MARGIN:-MARGIN]
    width = inner.shape[2]
    first_part = inner[:, :, :MARGIN] + from_prev
    middle_part = inner[:, :, MARGIN : width - MARGIN]
    last_part = inner[:, :, width - MARGIN :] + from_next
    return jnp.concatenate([first_part, middle_part, last_part], axis=2)


def fold_row_margins(gradient):
    low_rim = gradient[:, :MARGIN, :]
    high_rim = gradient[:, -MARGIN:, :]
    from_next = passed_along(low_rim, "row", -1)
    from_prev = passed_along(high_rim, "row", 1)
    inner = gradient[:, MARGIN:-MARGIN, :]
    height = inner.shape[1]
    first_part = inner[:, :MARGIN, :] + from_prev
    middle_part = inner[:, MARGIN : height - MARGIN, :]
    last_part = inner[:, height - MARGIN :, :] + from_next
    return jnp.concatenate([first_part, middle_part, last_part], axis=1)


def shards(object_field, probe, amplitudes, offsets, counts):
    measured = amplitudes[0, 0]
    offset_list = offsets[0, 0]
    live_count = counts[0, 0]
    current = object_field
    for sweep in range(PASSES):
        tile_field = object_rim(current)
        gradient = tile_gradient(tile_field, probe, measured, offset_list, live_count)
        summed = fold_row_margins(fold_col_margins(gradient))
        current = current + step_size * summed
    return current


def solution(mesh):
    return jax.shard_map(
        shards,
        mesh=mesh,
        in_specs=(
            P(None, "row", "col"),
            P(),
            P("row", "col", None, None, None),
            P("row", "col", None, None),
            P("row", "col"),
        ),
        out_specs=P(None, "row", "col"),
        check_vma=False,
    )
```

profile of v0, /device:TPU:14, one launch (start us, length us, event | category | flops | bytes accessed | tf_op | source)
XLA Modules:
  0.0 468.2 jit_solution(8523896160831342569)
XLA Ops:
  3.3 4.5 collective-permute-start.1
  12.7 5.2 %collective-permute-start.2 = (f32[2,48,384]{2,1,0:T(8,128)S(1)}, f32[2,48,384]{2,1,0:T(8,128)S(1)}, u32[]{:S(2)}, u32[]{:S(2)}) collective-permute-start(f32[2,48,384]{2,1,0:T(8,128)S(1)} %get-tuple-element.235), channel_id=1, source_target_pairs={{0,1},{1,2},{2,3},{3,4},{4,5},{5,6},{6,7},{7,8},{8,9},{9,10},{10,1... | collective-permute-start | bytes 442376 | tf_op jit(solution)/shard_map/ppermute | solution.py:23
  17.9 5.4 %collective-permute-start.3 = (f32[2,48,384]{2,1,0:T(8,128)S(1)}, f32[2,48,384]{2,1,0:T(8,128)}, u32[]{:S(2)}, u32[]{:S(2)}) collective-permute-start(f32[2,48,384]{2,1,0:T(8,128)S(1)} %get-tuple-element.236), channel_id=1, source_target_pairs={{1,0},{2,1},{3,2},{4,3},{5,4},{6,5},{7,6},{8,7},{9,8},{10,9},{11,1... | collective-permute-start | bytes 442376 | tf_op jit(solution)/shard_map/ppermute | solution.py:24
  27.2 5.0 %collective-permute-done.3 = f32[2,48,384]{2,1,0:T(8,128)} collective-permute-done((f32[2,48,384]{2,1,0:T(8,128)S(1)}, f32[2,48,384]{2,1,0:T(8,128)}, u32[]{:S(2)}, u32[]{:S(2)}) %collective-permute-start.3) | collective-permute-done | bytes 147488 | tf_op jit(solution)/shard_map/ppermute | solution.py:24
  33.5 2.4 broadcast.266.clone
  36.0 23.5 %while.30 = (s32[]{:T(128)}, f32[2,384,384]{2,1,0:T(8,128)S(1)}, s32[8,3]{0,1:T(4,128)S(1)}, f32[8,2,256,256]{3,2,1,0:T(8,128)}, s32[]{:T(128)}) while((s32[]{:T(128)}, f32[2,384,384]{2,1,0:T(8,128)S(1)}, s32[8,3]{0,1:T(4,128)S(1)}, f32[8,2,256,256]{3,2,1,0:T(8,128)}, s32[]{:T(128)}) %tuple.104), condition=%wide.while_cond, body=%wide.while_body.sunk | while | flops 2 | bytes 1050217 | solution.py:58
  42.5 2.3 bitcast_dynamic-update-slice_fusion.4
  48.4 2.3 bitcast_dynamic-update-slice_fusion.4
  54.2 2.3 bitcast_dynamic-update-slice_fusion.4
  57.1 2.3 bitcast_dynamic-update-slice_fusion.4
  59.4 4.2 subtract_convert_fusion.1
  63.7 6.0 %convolution_bitcast_fusion.3 = f32[8,2,256,256]{3,2,1,0:T(8,128)} fusion(bf16[8,1,256,256]{3,2,1,0:T(8,128)(2,1)} %get-tuple-element.228, bf16[8,1,256,256]{3,2,1,0:T(8,128)(2,1)} %get-tuple-element.227, bf16[1,2,256,256]{3,2,1,0:T(8,128)(2,1)S(1)} %copy-done.8, bf16[1,2,256,256]{3,2,1,0:T(8,128)(2,1)S(1)} %copy-done.10), kind=kOutput, calls=%fused_computation.21 | convolution fusion | flops 2154823680 | bytes 6815744 | tf_op jit(solution)/shard_map/cdkn,pdmn->pcmk/dot_general | solution.py:52
  69.6 4.2 fusion.2
  73.9 7.3 %convolution_bitcast_fusion.2 = f32[8,2,256,256]{3,2,1,0:T(8,128)} fusion(f32[8,2,256,256]{3,2,1,0:T(8,128)} %convolution_bitcast_fusion.3, f32[8,256,256]{2,1,0:T(8,128)} %fusion.2, bf16[1,2,256,256]{3,2,1,0:T(8,128)(2,1)S(1)} %copy-done.6, bf16[1,2,256,256]{3,2,1,0:T(8,128)(2,1)S(1)} %copy-done.4), kind=kOutput, calls=%fused_computation.20 | convolution fusion | flops 2152726528 | bytes 11010048 | tf_op jit(solution)/shard_map/cdkn,pdmn->pcmk/dot_general | solution.py:52
  81.2 2.8 multiply_add_fusion.1
  84.0 2.4 pad_maximum_fusion
  86.4 103.8 %while.28 = (s32[]{:T(128)}, f32[2,384,384]{2,1,0:T(8,128)S(1)}, s32[8,2]{0,1:T(2,128)S(1)}, f32[8,2,256,256]{3,2,1,0:T(8,128)}, s32[]{:T(128)}, /*index=5*/s32[]{:T(128)}, s32[]{:T(128)}) while((s32[]{:T(128)}, f32[2,384,384]{2,1,0:T(8,128)S(1)}, s32[8,2]{0,1:T(2,128)S(1)}, f32[8,2,256,256]{3,2,1,0:T(8,128)}, s32[]{:T(128)}, ...), condition=%wide.region_1.2_spmd, body=%wide.region_0.1_spmd.sunk | while | flops 131080 | bytes 2621637 | solution.py:109
  92.1 8.1 %dynamic_update_slice.16 = f32[2,384,384]{2,1,0:T(8,128)S(1)} dynamic-update-slice(f32[2,384,384]{2,1,0:T(8,128)S(1)} %get-tuple-element.396, f32[2,256,256]{2,1,0:T(8,128)S(1)} %bitcast_add_fusion.4, s32[]{:T(128)} %constant.90.clone.1..sunk, s32[]{:T(128)S(6)} %select_n.130, s32[]{:T(128)S(6)} %select_n.131) | dynamic-update-slice | bytes 1048580 | tf_op jit(solution)/shard_map/while/body/eval_jaxpr/dynamic_update_slice | solution.py:93
  106.0 8.1 %dynamic_update_slice.16 = f32[2,384,384]{2,1,0:T(8,128)S(1)} dynamic-update-slice(f32[2,384,384]{2,1,0:T(8,128)S(1)} %get-tuple-element.396, f32[2,256,256]{2,1,0:T(8,128)S(1)} %bitcast_add_fusion.4, s32[]{:T(128)} %constant.90.clone.1..sunk, s32[]{:T(128)S(6)} %select_n.130, s32[]{:T(128)S(6)} %select_n.131) | dynamic-update-slice | bytes 1048580 | tf_op jit(solution)/shard_map/while/body/eval_jaxpr/dynamic_update_slice | solution.py:93
  119.8 5.6 %dynamic_update_slice.16 = f32[2,384,384]{2,1,0:T(8,128)S(1)} dynamic-update-slice(f32[2,384,384]{2,1,0:T(8,128)S(1)} %get-tuple-element.396, f32[2,256,256]{2,1,0:T(8,128)S(1)} %bitcast_add_fusion.4, s32[]{:T(128)} %constant.90.clone.1..sunk, s32[]{:T(128)S(6)} %select_n.130, s32[]{:T(128)S(6)} %select_n.131) | dynamic-update-slice | bytes 1048580 | tf_op jit(solution)/shard_map/while/body/eval_jaxpr/dynamic_update_slice | solution.py:93
  131.2 7.0 %dynamic_update_slice.16 = f32[2,384,384]{2,1,0:T(8,128)S(1)} dynamic-update-slice(f32[2,384,384]{2,1,0:T(8,128)S(1)} %get-tuple-element.396, f32[2,256,256]{2,1,0:T(8,128)S(1)} %bitcast_add_fusion.4, s32[]{:T(128)} %constant.90.clone.1..sunk, s32[]{:T(128)S(6)} %select_n.130, s32[]{:T(128)S(6)} %select_n.131) | dynamic-update-slice | bytes 1048580 | tf_op jit(solution)/shard_map/while/body/eval_jaxpr/dynamic_update_slice | solution.py:93
  143.9 7.2 %dynamic_update_slice.16 = f32[2,384,384]{2,1,0:T(8,128)S(1)} dynamic-update-slice(f32[2,384,384]{2,1,0:T(8,128)S(1)} %get-tuple-element.396, f32[2,256,256]{2,1,0:T(8,128)S(1)} %bitcast_add_fusion.4, s32[]{:T(128)} %constant.90.clone.1..sunk, s32[]{:T(128)S(6)} %select_n.130, s32[]{:T(128)S(6)} %select_n.131) | dynamic-update-slice | bytes 1048580 | tf_op jit(solution)/shard_map/while/body/eval_jaxpr/dynamic_update_slice | solution.py:93
  156.8 7.3 %dynamic_update_slice.16 = f32[2,384,384]{2,1,0:T(8,128)S(1)} dynamic-update-slice(f32[2,384,384]{2,1,0:T(8,128)S(1)} %get-tuple-element.396, f32[2,256,256]{2,1,0:T(8,128)S(1)} %bitcast_add_fusion.4, s32[]{:T(128)} %constant.90.clone.1..sunk, s32[]{:T(128)S(6)} %select_n.130, s32[]{:T(128)S(6)} %select_n.131) | dynamic-update-slice | bytes 1048580 | tf_op jit(solution)/shard_map/while/body/eval_jaxpr/dynamic_update_slice | solution.py:93
  169.8 7.2 %dynamic_update_slice.16 = f32[2,384,384]{2,1,0:T(8,128)S(1)} dynamic-update-slice(f32[2,384,384]{2,1,0:T(8,128)S(1)} %get-tuple-element.396, f32[2,256,256]{2,1,0:T(8,128)S(1)} %bitcast_add_fusion.4, s32[]{:T(128)} %constant.90.clone.1..sunk, s32[]{:T(128)S(6)} %select_n.130, s32[]{:T(128)S(6)} %select_n.131) | dynamic-update-slice | bytes 1048580 | tf_op jit(solution)/shard_map/while/body/eval_jaxpr/dynamic_update_slice | solution.py:93
  182.7 7.6 %dynamic_update_slice.16 = f32[2,384,384]{2,1,0:T(8,128)S(1)} dynamic-update-slice(f32[2,384,384]{2,1,0:T(8,128)S(1)} %get-tuple-element.396, f32[2,256,256]{2,1,0:T(8,128)S(1)} %bitcast_add_fusion.4, s32[]{:T(128)} %constant.90.clone.1..sunk, s32[]{:T(128)S(6)} %select_n.130, s32[]{:T(128)S(6)} %select_n.131) | dynamic-update-slice | bytes 1048580 | tf_op jit(solution)/shard_map/while/body/eval_jaxpr/dynamic_update_slice | solution.py:93
  190.5 3.5 collective-permute-start.4
  194.0 6.4 %collective-permute-done.4 = f32[2,384,48]{2,1,0:T(8,128)S(1)} collective-permute-done((f32[2,384,48]{2,1,0:T(8,128)S(1)}, f32[2,384,48]{2,1,0:T(8,128)S(1)}, u32[]{:S(2)}, u32[]{:S(2)}) %collective-permute-start.4) | collective-permute-done | bytes 147488 | tf_op jit(solution)/shard_map/ppermute | solution.py:32
  202.8 5.0 %collective-permute-done.5 = f32[2,384,48]{2,1,0:T(8,128)S(1)} collective-permute-done((f32[2,384,48]{2,1,0:T(8,128)S(1)}, f32[2,384,48]{2,1,0:T(8,128)S(1)}, u32[]{:S(2)}, u32[]{:S(2)}) %collective-permute-start.5) | collective-permute-done | bytes 147488 | tf_op jit(solution)/shard_map/ppermute | solution.py:32
  208.2 9.2 %collective-permute-start.6 = (f32[2,48,288]{2,1,0:T(8,128)S(1)}, f32[2,48,288]{2,1,0:T(8,128)S(1)}, u32[]{:S(2)}, u32[]{:S(2)}) collective-permute-start(f32[2,48,288]{2,1,0:T(8,128)S(1)} %pad_maximum_fusion.16), channel_id=1, source_target_pairs={{0,1},{1,2},{2,3},{3,4},{4,5},{5,6},{6,7},{7,8},{8,9},{9,10},{10,1... | collective-permute-start | bytes 331784 | tf_op jit(solution)/shard_map/ppermute | solution.py:32
  217.3 6.0 %collective-permute-done.6 = f32[2,48,288]{2,1,0:T(8,128)S(1)} collective-permute-done((f32[2,48,288]{2,1,0:T(8,128)S(1)}, f32[2,48,288]{2,1,0:T(8,128)S(1)}, u32[]{:S(2)}, u32[]{:S(2)}) %collective-permute-start.6) | collective-permute-done | bytes 110624 | tf_op jit(solution)/shard_map/ppermute | solution.py:32
  223.5 4.6 collective-permute-start.7
  228.7 4.6 collective-permute-done.7
  235.7 4.5 collective-permute-start.9
  240.2 3.5 collective-permute-done.8
  244.6 3.8 collective-permute-start.10
  248.4 5.3 %collective-permute-start.11 = (f32[2,48,384]{2,1,0:T(8,128)S(1)}, f32[2,48,384]{2,1,0:T(8,128)}, u32[]{:S(2)}, u32[]{:S(2)}) collective-permute-start(f32[2,48,384]{2,1,0:T(8,128)S(1)} %get-tuple-element.234), channel_id=1, source_target_pairs={{1,0},{2,1},{3,2},{4,3},{5,4},{6,5},{7,6},{8,7},{9,8},{10,9},{11,1... | collective-permute-start | bytes 442376 | tf_op jit(solution)/shard_map/ppermute | solution.py:24
  253.7 4.9 %collective-permute-done.10 = f32[2,48,384]{2,1,0:T(8,128)S(1)} collective-permute-done((f32[2,48,384]{2,1,0:T(8,128)S(1)}, f32[2,48,384]{2,1,0:T(8,128)S(1)}, u32[]{:S(2)}, u32[]{:S(2)}) %collective-permute-start.10) | collective-permute-done | bytes 147488 | tf_op jit(solution)/shard_map/ppermute | solution.py:23
  261.7 2.4 broadcast.266
  264.1 23.5 %while.31 = (s32[]{:T(128)}, f32[2,384,384]{2,1,0:T(8,128)S(1)}, s32[8,3]{0,1:T(4,128)S(1)}, f32[8,2,256,256]{3,2,1,0:T(8,128)}, s32[]{:T(128)}) while((s32[]{:T(128)}, f32[2,384,384]{2,1,0:T(8,128)S(1)}, s32[8,3]{0,1:T(4,128)S(1)}, f32[8,2,256,256]{3,2,1,0:T(8,128)}, s32[]{:T(128)}) %tuple.116), condition=%wide.while_cond.1, body=%wide.while_body.1.sunk | while | flops 2 | bytes 1050217 | solution.py:58
  270.6 2.3 bitcast_dynamic-update-slice_fusion.5
  276.5 2.3 bitcast_dynamic-update-slice_fusion.5
  285.3 2.3 bitcast_dynamic-update-slice_fusion.5
  287.6 4.2 subtract_convert_fusion
  291.8 6.0 %convolution_bitcast_fusion.1 = f32[8,2,256,256]{3,2,1,0:T(8,128)} fusion(bf16[8,1,256,256]{3,2,1,0:T(8,128)(2,1)} %get-tuple-element.224, bf16[8,1,256,256]{3,2,1,0:T(8,128)(2,1)} %get-tuple-element.223, bf16[1,2,256,256]{3,2,1,0:T(8,128)(2,1)S(1)} %copy-done.9, bf16[1,2,256,256]{3,2,1,0:T(8,128)(2,1)S(1)} %copy-done.11), kind=kOutput, calls=%fused_computation.19 | convolution fusion | flops 2154823680 | bytes 6815744 | tf_op jit(solution)/shard_map/cdkn,pdmn->pcmk/dot_general | solution.py:52
  297.8 4.2 fusion.5
  302.0 7.3 %convolution_bitcast_fusion = f32[8,2,256,256]{3,2,1,0:T(8,128)} fusion(f32[8,2,256,256]{3,2,1,0:T(8,128)} %convolution_bitcast_fusion.1, f32[8,256,256]{2,1,0:T(8,128)} %fusion.5, bf16[1,2,256,256]{3,2,1,0:T(8,128)(2,1)S(1)} %copy-done.7, bf16[1,2,256,256]{3,2,1,0:T(8,128)(2,1)S(1)} %copy-done.5), kind=kOutput, calls=%fused_computation.18 | convolution fusion | flops 2152726528 | bytes 11010048 | tf_op jit(solution)/shard_map/cdkn,pdmn->pcmk/dot_general | solution.py:52
  309.4 2.8 multiply_add_fusion
  312.1 2.4 pad_maximum_fusion.1
  314.6 104.1 %while.29 = (s32[]{:T(128)}, f32[2,384,384]{2,1,0:T(8,128)S(1)}, s32[8,2]{0,1:T(2,128)S(1)}, f32[8,2,256,256]{3,2,1,0:T(8,128)}, s32[]{:T(128)}, /*index=5*/s32[]{:T(128)}, s32[]{:T(128)}) while((s32[]{:T(128)}, f32[2,384,384]{2,1,0:T(8,128)S(1)}, s32[8,2]{0,1:T(2,128)S(1)}, f32[8,2,256,256]{3,2,1,0:T(8,128)}, s32[]{:T(128)}, ...), condition=%wide.region_3.4_spmd, body=%wide.region_2.3_spmd.sunk | while | flops 131080 | bytes 2621637 | solution.py:109
  320.3 8.1 %dynamic_update_slice.17 = f32[2,384,384]{2,1,0:T(8,128)S(1)} dynamic-update-slice(f32[2,384,384]{2,1,0:T(8,128)S(1)} %get-tuple-element.432, f32[2,256,256]{2,1,0:T(8,128)S(1)} %bitcast_add_fusion.5, s32[]{:T(128)} %constant.90.clone.1..sunk.1, s32[]{:T(128)S(6)} %select_n.132, s32[]{:T(128)S(6)} %select_n.133) | dynamic-update-slice | bytes 1048580 | tf_op jit(solution)/shard_map/while/body/eval_jaxpr/dynamic_update_slice | solution.py:93
  334.2 8.1 %dynamic_update_slice.17 = f32[2,384,384]{2,1,0:T(8,128)S(1)} dynamic-update-slice(f32[2,384,384]{2,1,0:T(8,128)S(1)} %get-tuple-element.432, f32[2,256,256]{2,1,0:T(8,128)S(1)} %bitcast_add_fusion.5, s32[]{:T(128)} %constant.90.clone.1..sunk.1, s32[]{:T(128)S(6)} %select_n.132, s32[]{:T(128)S(6)} %select_n.133) | dynamic-update-slice | bytes 1048580 | tf_op jit(solution)/shard_map/while/body/eval_jaxpr/dynamic_update_slice | solution.py:93
  348.1 5.6 %dynamic_update_slice.17 = f32[2,384,384]{2,1,0:T(8,128)S(1)} dynamic-update-slice(f32[2,384,384]{2,1,0:T(8,128)S(1)} %get-tuple-element.432, f32[2,256,256]{2,1,0:T(8,128)S(1)} %bitcast_add_fusion.5, s32[]{:T(128)} %constant.90.clone.1..sunk.1, s32[]{:T(128)S(6)} %select_n.132, s32[]{:T(128)S(6)} %select_n.133) | dynamic-update-slice | bytes 1048580 | tf_op jit(solution)/shard_map/while/body/eval_jaxpr/dynamic_update_slice | solution.py:93
  359.5 7.0 %dynamic_update_slice.17 = f32[2,384,384]{2,1,0:T(8,128)S(1)} dynamic-update-slice(f32[2,384,384]{2,1,0:T(8,128)S(1)} %get-tuple-element.432, f32[2,256,256]{2,1,0:T(8,128)S(1)} %bitcast_add_fusion.5, s32[]{:T(128)} %constant.90.clone.1..sunk.1, s32[]{:T(128)S(6)} %select_n.132, s32[]{:T(128)S(6)} %select_n.133) | dynamic-update-slice | bytes 1048580 | tf_op jit(solution)/shard_map/while/body/eval_jaxpr/dynamic_update_slice | solution.py:93
  372.2 7.2 %dynamic_update_slice.17 = f32[2,384,384]{2,1,0:T(8,128)S(1)} dynamic-update-slice(f32[2,384,384]{2,1,0:T(8,128)S(1)} %get-tuple-element.432, f32[2,256,256]{2,1,0:T(8,128)S(1)} %bitcast_add_fusion.5, s32[]{:T(128)} %constant.90.clone.1..sunk.1, s32[]{:T(128)S(6)} %select_n.132, s32[]{:T(128)S(6)} %select_n.133) | dynamic-update-slice | bytes 1048580 | tf_op jit(solution)/shard_map/while/body/eval_jaxpr/dynamic_update_slice | solution.py:93
  385.2 7.3 %dynamic_update_slice.17 = f32[2,384,384]{2,1,0:T(8,128)S(1)} dynamic-update-slice(f32[2,384,384]{2,1,0:T(8,128)S(1)} %get-tuple-element.432, f32[2,256,256]{2,1,0:T(8,128)S(1)} %bitcast_add_fusion.5, s32[]{:T(128)} %constant.90.clone.1..sunk.1, s32[]{:T(128)S(6)} %select_n.132, s32[]{:T(128)S(6)} %select_n.133) | dynamic-update-slice | bytes 1048580 | tf_op jit(solution)/shard_map/while/body/eval_jaxpr/dynamic_update_slice | solution.py:93
  398.2 7.2 %dynamic_update_slice.17 = f32[2,384,384]{2,1,0:T(8,128)S(1)} dynamic-update-slice(f32[2,384,384]{2,1,0:T(8,128)S(1)} %get-tuple-element.432, f32[2,256,256]{2,1,0:T(8,128)S(1)} %bitcast_add_fusion.5, s32[]{:T(128)} %constant.90.clone.1..sunk.1, s32[]{:T(128)S(6)} %select_n.132, s32[]{:T(128)S(6)} %select_n.133) | dynamic-update-slice | bytes 1048580 | tf_op jit(solution)/shard_map/while/body/eval_jaxpr/dynamic_update_slice | solution.py:93
  411.1 7.6 %dynamic_update_slice.17 = f32[2,384,384]{2,1,0:T(8,128)S(1)} dynamic-update-slice(f32[2,384,384]{2,1,0:T(8,128)S(1)} %get-tuple-element.432, f32[2,256,256]{2,1,0:T(8,128)S(1)} %bitcast_add_fusion.5, s32[]{:T(128)} %constant.90.clone.1..sunk.1, s32[]{:T(128)S(6)} %select_n.132, s32[]{:T(128)S(6)} %select_n.133) | dynamic-update-slice | bytes 1048580 | tf_op jit(solution)/shard_map/while/body/eval_jaxpr/dynamic_update_slice | solution.py:93
  418.9 3.4 collective-permute-start.12
  422.3 6.6 %collective-permute-done.12 = f32[2,384,48]{2,1,0:T(8,128)S(1)} collective-permute-done((f32[2,384,48]{2,1,0:T(8,128)S(1)}, f32[2,384,48]{2,1,0:T(8,128)S(1)}, u32[]{:S(2)}, u32[]{:S(2)}) %collective-permute-start.12) | collective-permute-done | bytes 147488 | tf_op jit(solution)/shard_map/ppermute | solution.py:32
  431.3 5.0 %collective-permute-done.13 = f32[2,384,48]{2,1,0:T(8,128)S(1)} collective-permute-done((f32[2,384,48]{2,1,0:T(8,128)S(1)}, f32[2,384,48]{2,1,0:T(8,128)S(1)}, u32[]{:S(2)}, u32[]{:S(2)}) %collective-permute-start.13) | collective-permute-done | bytes 147488 | tf_op jit(solution)/shard_map/ppermute | solution.py:32
  436.6 7.4 %collective-permute-start.14 = (f32[2,48,288]{2,1,0:T(8,128)S(1)}, f32[2,48,288]{2,1,0:T(8,128)S(1)}, u32[]{:S(2)}, u32[]{:S(2)}) collective-permute-start(f32[2,48,288]{2,1,0:T(8,128)S(1)} %pad_maximum_fusion.11), channel_id=1, source_target_pairs={{0,1},{1,2},{2,3},{3,4},{4,5},{5,6},{6,7},{7,8},{8,9},{9,10},{10,1... | collective-permute-start | bytes 331784 | tf_op jit(solution)/shard_map/ppermute | solution.py:32
  444.0 14.9 %collective-permute-done.14 = f32[2,48,288]{2,1,0:T(8,128)S(1)} collective-permute-done((f32[2,48,288]{2,1,0:T(8,128)S(1)}, f32[2,48,288]{2,1,0:T(8,128)S(1)}, u32[]{:S(2)}, u32[]{:S(2)}) %collective-permute-start.14) | collective-permute-done | bytes 110624 | tf_op jit(solution)/shard_map/ppermute | solution.py:32
  459.1 4.8 %collective-permute-start.15 = (f32[2,48,288]{2,1,0:T(8,128)S(1)}, f32[2,48,288]{2,1,0:T(8,128)S(1)}, u32[]{:S(2)}, u32[]{:S(2)}) collective-permute-start(f32[2,48,288]{2,1,0:T(8,128)S(1)} %get-tuple-element.230), channel_id=1, source_target_pairs={{1,0},{2,1},{3,2},{4,3},{5,4},{6,5},{7,6},{8,7},{9,8},{10,9},{11,1... | collective-permute-start | bytes 331784 | tf_op jit(solution)/shard_map/ppermute | solution.py:32
  464.6 2.5 collective-permute-done.15
  (163 shorter events, 88.4 us)
Async XLA Ops:
  0.0 12.5 %copy-start = (f32[2,288,288]{2,1,0:T(8,128)S(1)}, f32[2,288,288]{2,1,0:T(8,128)}, u32[]{:S(2)}) copy-start(f32[2,288,288]{2,1,0:T(8,128)} %param.9) | copy-start | bytes 1990660
  0.0 11.8 %copy-start.3 = (f32[2,256,256]{2,1,0:T(8,128)S(1)}, f32[2,256,256]{2,1,0:T(8,128)}, u32[]{:S(2)}) copy-start(f32[2,256,256]{2,1,0:T(8,128)} %param.10) | copy-start | bytes 1572868
  1.4 11.1 %collective-permute-start = (f32[2,288,48]{2,1,0:T(8,128)S(1)}, f32[2,288,48]{2,1,0:T(8,128)S(1)}, u32[]{:S(2)}, u32[]{:S(2)}) collective-permute-start(f32[2,288,48]{2,1,0:T(8,128)S(1)} %get-tuple-element.243), channel_id=1, source_target_pairs={{0,16},{16,32},{32,48},{48,64},{64,80},{80,96},{96,112},{112,128},... | collective-permute-start | bytes 331784 | tf_op jit(solution)/shard_map/ppermute | solution.py:23
  3.3 9.2 %collective-permute-start.1 = (f32[2,288,48]{2,1,0:T(8,128)S(1)}, f32[2,288,48]{2,1,0:T(8,128)S(1)}, u32[]{:S(2)}, u32[]{:S(2)}) collective-permute-start(f32[2,288,48]{2,1,0:T(8,128)S(1)} %get-tuple-element.244), channel_id=1, source_target_pairs={{16,0},{32,16},{48,32},{64,48},{80,64},{96,80},{112,96},{128,112},... | collective-permute-start | bytes 331784 | tf_op jit(solution)/shard_map/ppermute | solution.py:24
  12.7 13.9 %collective-permute-start.2 = (f32[2,48,384]{2,1,0:T(8,128)S(1)}, f32[2,48,384]{2,1,0:T(8,128)S(1)}, u32[]{:S(2)}, u32[]{:S(2)}) collective-permute-start(f32[2,48,384]{2,1,0:T(8,128)S(1)} %get-tuple-element.235), channel_id=1, source_target_pairs={{0,1},{1,2},{2,3},{3,4},{4,5},{5,6},{6,7},{7,8},{8,9},{9,10},{10,1... | collective-permute-start | bytes 442376 | tf_op jit(solution)/shard_map/ppermute | solution.py:23
  17.9 14.3 %collective-permute-start.3 = (f32[2,48,384]{2,1,0:T(8,128)S(1)}, f32[2,48,384]{2,1,0:T(8,128)}, u32[]{:S(2)}, u32[]{:S(2)}) collective-permute-start(f32[2,48,384]{2,1,0:T(8,128)S(1)} %get-tuple-element.236), channel_id=1, source_target_pairs={{1,0},{2,1},{3,2},{4,3},{5,4},{6,5},{7,6},{8,7},{9,8},{10,9},{11,1... | collective-permute-start | bytes 442376 | tf_op jit(solution)/shard_map/ppermute | solution.py:24
  26.5 0.7 copy-start.12
  59.4 4.2 copy-start.8
  59.4 4.2 copy-start.10
  63.7 6.0 %copy-start.1 = (bf16[1,1,8,256,256]{4,3,2,1,0:T(8,128)(2,1)S(1)}, bf16[1,1,8,256,256]{4,3,2,1,0:T(8,128)(2,1)}, u32[]{:S(2)}) copy-start(bf16[1,1,8,256,256]{4,3,2,1,0:T(8,128)(2,1)} %param.11) | copy-start | bytes 3145732
  69.6 4.2 copy-start.4
  69.6 4.2 copy-start.6
  84.0 2.5 copy-start.13
  190.5 10.0 %collective-permute-start.4 = (f32[2,384,48]{2,1,0:T(8,128)S(1)}, f32[2,384,48]{2,1,0:T(8,128)S(1)}, u32[]{:S(2)}, u32[]{:S(2)}) collective-permute-start(f32[2,384,48]{2,1,0:T(8,128)S(1)} %slice.211), channel_id=1, source_target_pairs={{0,16},{16,32},{32,48},{48,64},{64,80},{80,96},{96,112},{112,128},... | collective-permute-start | bytes 442376 | tf_op jit(solution)/shard_map/ppermute | solution.py:32
  200.6 7.2 %collective-permute-start.5 = (f32[2,384,48]{2,1,0:T(8,128)S(1)}, f32[2,384,48]{2,1,0:T(8,128)S(1)}, u32[]{:S(2)}, u32[]{:S(2)}) collective-permute-start(f32[2,384,48]{2,1,0:T(8,128)S(1)} %get-tuple-element.240), channel_id=1, source_target_pairs={{16,0},{32,16},{48,32},{64,48},{80,64},{96,80},{112,96},{128,112},... | collective-permute-start | bytes 442376 | tf_op jit(solution)/shard_map/ppermute | solution.py:32
  208.2 15.2 %collective-permute-start.6 = (f32[2,48,288]{2,1,0:T(8,128)S(1)}, f32[2,48,288]{2,1,0:T(8,128)S(1)}, u32[]{:S(2)}, u32[]{:S(2)}) collective-permute-start(f32[2,48,288]{2,1,0:T(8,128)S(1)} %pad_maximum_fusion.16), channel_id=1, source_target_pairs={{0,1},{1,2},{2,3},{3,4},{4,5},{5,6},{6,7},{7,8},{8,9},{9,10},{10,1... | collective-permute-start | bytes 331784 | tf_op jit(solution)/shard_map/ppermute | solution.py:32
  223.5 9.8 %collective-permute-start.7 = (f32[2,48,288]{2,1,0:T(8,128)S(1)}, f32[2,48,288]{2,1,0:T(8,128)S(1)}, u32[]{:S(2)}, u32[]{:S(2)}) collective-permute-start(f32[2,48,288]{2,1,0:T(8,128)S(1)} %get-tuple-element.232), channel_id=1, source_target_pairs={{1,0},{2,1},{3,2},{4,3},{5,4},{6,5},{7,6},{8,7},{9,8},{10,9},{11,1... | collective-permute-start | bytes 331784 | tf_op jit(solution)/shard_map/ppermute | solution.py:32
  233.7 10.0 %collective-permute-start.8 = (f32[2,288,48]{2,1,0:T(8,128)S(1)}, f32[2,288,48]{2,1,0:T(8,128)S(1)}, u32[]{:S(2)}, u32[]{:S(2)}) collective-permute-start(f32[2,288,48]{2,1,0:T(8,128)S(1)} %get-tuple-element.241), channel_id=1, source_target_pairs={{0,16},{16,32},{32,48},{48,64},{64,80},{80,96},{96,112},{112,128},... | collective-permute-start | bytes 331784 | tf_op jit(solution)/shard_map/ppermute | solution.py:23
  235.7 8.8 %collective-permute-start.9 = (f32[2,288,48]{2,1,0:T(8,128)S(1)}, f32[2,288,48]{2,1,0:T(8,128)S(1)}, u32[]{:S(2)}, u32[]{:S(2)}) collective-permute-start(f32[2,288,48]{2,1,0:T(8,128)S(1)} %get-tuple-element.242), channel_id=1, source_target_pairs={{16,0},{32,16},{48,32},{64,48},{80,64},{96,80},{112,96},{128,112},... | collective-permute-start | bytes 331784 | tf_op jit(solution)/shard_map/ppermute | solution.py:24
  244.6 14.0 %collective-permute-start.10 = (f32[2,48,384]{2,1,0:T(8,128)S(1)}, f32[2,48,384]{2,1,0:T(8,128)S(1)}, u32[]{:S(2)}, u32[]{:S(2)}) collective-permute-start(f32[2,48,384]{2,1,0:T(8,128)S(1)} %get-tuple-element.233), channel_id=1, source_target_pairs={{0,1},{1,2},{2,3},{3,4},{4,5},{5,6},{6,7},{7,8},{8,9},{9,10},{10,1... | collective-permute-start | bytes 442376 | tf_op jit(solution)/shard_map/ppermute | solution.py:23
  248.4 12.0 %collective-permute-start.11 = (f32[2,48,384]{2,1,0:T(8,128)S(1)}, f32[2,48,384]{2,1,0:T(8,128)}, u32[]{:S(2)}, u32[]{:S(2)}) collective-permute-start(f32[2,48,384]{2,1,0:T(8,128)S(1)} %get-tuple-element.234), channel_id=1, source_target_pairs={{1,0},{2,1},{3,2},{4,3},{5,4},{6,5},{7,6},{8,7},{9,8},{10,9},{11,1... | collective-permute-start | bytes 442376 | tf_op jit(solution)/shard_map/ppermute | solution.py:24
  287.6 4.2 copy-start.9
  287.6 4.2 copy-start.11
  291.8 6.0 %copy-start.2 = (bf16[1,1,8,256,256]{4,3,2,1,0:T(8,128)(2,1)S(1)}, bf16[1,1,8,256,256]{4,3,2,1,0:T(8,128)(2,1)}, u32[]{:S(2)}) copy-start(bf16[1,1,8,256,256]{4,3,2,1,0:T(8,128)(2,1)} %param.11) | copy-start | bytes 3145732
  297.8 4.2 copy-start.5
  297.8 4.2 copy-start.7
  418.9 10.0 %collective-permute-start.12 = (f32[2,384,48]{2,1,0:T(8,128)S(1)}, f32[2,384,48]{2,1,0:T(8,128)S(1)}, u32[]{:S(2)}, u32[]{:S(2)}) collective-permute-start(f32[2,384,48]{2,1,0:T(8,128)S(1)} %slice.231), channel_id=1, source_target_pairs={{0,16},{16,32},{32,48},{48,64},{64,80},{80,96},{96,112},{112,128},... | collective-permute-start | bytes 442376 | tf_op jit(solution)/shard_map/ppermute | solution.py:32
  429.1 7.2 %collective-permute-start.13 = (f32[2,384,48]{2,1,0:T(8,128)S(1)}, f32[2,384,48]{2,1,0:T(8,128)S(1)}, u32[]{:S(2)}, u32[]{:S(2)}) collective-permute-start(f32[2,384,48]{2,1,0:T(8,128)S(1)} %get-tuple-element.238), channel_id=1, source_target_pairs={{16,0},{32,16},{48,32},{64,48},{80,64},{96,80},{112,96},{128,112},... | collective-permute-start | bytes 442376 | tf_op jit(solution)/shard_map/ppermute | solution.py:32
  436.6 22.4 %collective-permute-start.14 = (f32[2,48,288]{2,1,0:T(8,128)S(1)}, f32[2,48,288]{2,1,0:T(8,128)S(1)}, u32[]{:S(2)}, u32[]{:S(2)}) collective-permute-start(f32[2,48,288]{2,1,0:T(8,128)S(1)} %pad_maximum_fusion.11), channel_id=1, source_target_pairs={{0,1},{1,2},{2,3},{3,4},{4,5},{5,6},{6,7},{7,8},{8,9},{9,10},{10,1... | collective-permute-start | bytes 331784 | tf_op jit(solution)/shard_map/ppermute | solution.py:32
  459.1 7.9 %collective-permute-start.15 = (f32[2,48,288]{2,1,0:T(8,128)S(1)}, f32[2,48,288]{2,1,0:T(8,128)S(1)}, u32[]{:S(2)}, u32[]{:S(2)}) collective-permute-start(f32[2,48,288]{2,1,0:T(8,128)S(1)} %get-tuple-element.230), channel_id=1, source_target_pairs={{1,0},{2,1},{3,2},{4,3},{5,4},{6,5},{7,6},{8,7},{9,8},{10,9},{11,1... | collective-permute-start | bytes 331784 | tf_op jit(solution)/shard_map/ppermute | solution.py:32
where the time goes:
time: 470 us; the launch traced here: 468 us
  local copies, waits for them, and re-layouts  181 us (39%)
  starting transfers between devices  69.3 us (15%)
  waiting for transfers between devices  69.3 us (15%)
  loops' own time  61.7 us (13%)
  other arithmetic  59 us (13%)
  matrix products  26.6 us (6%)
    dynamic_update_slice x16, local copies, waits for them, and re-layouts, add_patch(): return lax.dynamic_update_slice(current, existing + term, start)  116 us
    another operation x2, loops' own time, tile_gradient(): return lax.fori_loop(0, offset_list.shape[0], add_slot, zeros_tile)  61.7 us
    ppermute x8, waiting for transfers between devices, passed_along(): lax.ppermute(value, axis, [(source, source + steps) for source in range(f...  51.1 us
    gather x48, local copies, waits for them, and re-layouts  46.9 us
    ppermute x8, starting transfers between devices, passed_along(): lax.ppermute(value, axis, [(source, source + steps) for source in range(f...  36.7 us
    dot_general x4, matrix products, transform(): jnp.einsum('cdkn,pdmn->pcmk', table, first, preferred_element_type=jnp.fl...  26.6 us
    add x16, other arithmetic, add_patch(): return lax.dynamic_update_slice(current, existing + term, start)  20.1 us
    ppermute x4, starting transfers between devices, with_halo(): after = lax.ppermute(first, axis, down)  19.7 us
  transfers between devices with their start and end apart: 16, of which 14 were waited for; matrix products, arithmetic and copies ran while one was open for 1% of the time, Pallas kernels for 0%

commit v1 on v0

v1 whole, which is shorter than its diff:
```python
import functools
import math

import jax
import jax.numpy as jnp
import numpy as np
from jax import lax
from jax.experimental import pallas as pl
from jax.experimental.pallas import tpu as pltpu
from jax.sharding import PartitionSpec as P

MARGIN = 48
PASSES = 2
SIDE = 256
HALF = 128
CORE = 288
TILE = 384
SLOTS = 8
STEP = 0.1
FLOOR = 0.01
F32 = jnp.float32
BF16 = jnp.bfloat16

EDGE = ((0, 48), (80, 48))
INNER = ((48, 32), (128, 128))
N_EDGE = 96
N_INNER = 160


def half_tables():
    position = np.arange(SIDE)
    angle = (position[:, None] * position[None, :] % SIDE) * (2.0 * math.pi / SIDE)
    scale = 1.0 / math.sqrt(SIDE)
    cosine, sine = np.cos(angle) * scale, np.sin(angle) * scale
    table = np.concatenate([cosine[:HALF], cosine[HALF : HALF + 1], sine[1:HALF]])
    order = np.concatenate([np.arange(HALF), [HALF], np.arange(SIDE - 1, HALF, -1)])
    swap = np.zeros((SIDE, SIDE), np.float32)
    swap[np.arange(SIDE), order] = 1.0
    return [a.astype(jnp.bfloat16) for a in (table, table.T, swap)]


def mm(a, b):
    return jnp.dot(a, b, preferred_element_type=F32)


def lane_iota(rows):
    return lax.broadcasted_iota(jnp.int32, (rows, HALF), 1)


def row_iota(rows, start):
    return lax.broadcasted_iota(jnp.int32, (rows, HALF), 0) + start


def blk(n):
    return pl.ds(n * HALF, HALF)


def chunks(ranges, step):
    for start, length in ranges:
        for at in range(start, start + length, step):
            yield at


def kernel(
    off, cnt, obj, probe, amp, table, table_t, swap, out,
    ob, pb, ab, tv, ttv, sv,
    pr, ap, hb, wb, qb, xe, xi, cur, g,
    row_in, col_s, col_in, grow_s, grow_in, gcol_s, gcol_in, frow_s, frow_in, fcol_s, fcol_in,
    load_sem, send_sem, recv_sem,
):
    n_row, n_col = lax.axis_size("row"), lax.axis_size("col")
    me_r, me_c = lax.axis_index("row"), lax.axis_index("col")
    has = {("row", 0): me_r > 0, ("row", 1): me_r < n_row - 1, ("col", 0): me_c > 0, ("col", 1): me_c < n_col - 1}
    to = {("row", 0): me_r - 1, ("row", 1): me_r + 1, ("col", 0): me_c - 1, ("col", 1): me_c + 1}

    loads = [
        pltpu.make_async_copy(src, dst, load_sem.at[i])
        for i, (src, dst) in enumerate(
            ((obj, ob), (probe, pb), (amp, ab), (table, tv), (table_t, ttv), (swap, sv))
        )
    ]
    for copy in loads:
        copy.start()

    barrier = pltpu.get_barrier_semaphore()
    for key, ok in has.items():
        @pl.when(ok)
        def _(key=key):
            pl.semaphore_signal(barrier, inc=1, device_id={key[0]: to[key]}, device_id_type=pl.DeviceIdType.MESH)
    pl.semaphore_wait(barrier, sum(ok.astype(jnp.int32) for ok in has.values()))

    def remote(axis, side, number, src, dst):
        return pltpu.make_async_remote_copy(
            src_ref=src,
            dst_ref=dst,
            send_sem=send_sem.at[number * 2 + side],
            recv_sem=recv_sem.at[number * 2 + (1 - side)],
            device_id={axis: to[axis, side]},
            device_id_type=pl.DeviceIdType.MESH,
        )

    def send(axis, side, number, src, dst):
        @pl.when(has[axis, side])
        def _():
            remote(axis, side, number, src, dst).start()

    def sent(axis, side, number, src, dst):
        @pl.when(has[axis, side])
        def _():
            remote(axis, side, number, src, dst).wait_send()

    def arrived(axis, side, number, src, dst):
        @pl.when(has[axis, side])
        def _():
            pltpu.make_async_remote_copy(
                src_ref=src, dst_ref=dst,
                send_sem=send_sem.at[number * 2 + 1 - side],
                recv_sem=recv_sem.at[number * 2 + side],
                device_id={axis: to[axis, side]},
                device_id_type=pl.DeviceIdType.MESH,
            ).wait_recv()

    lanes8 = lane_iota(8)

    def halo_row(side):
        start = 0 if side == 0 else CORE - MARGIN
        return ob.at[:, pl.ds(start, MARGIN), :], row_in.at[1 - side]

    loads[0].wait()
    for side in (0, 1):
        send("row", side, 0, *halo_row(side))

    def place(comp, row, values):
        n = values[0].shape[0]
        lane = lane_iota(n)
        rolled = [pltpu.roll(v, MARGIN, 1) for v in values]
        cur[comp, pl.ds(row, n), blk(0)] = jnp.where(lane < MARGIN, 0.0, rolled[0])
        cur[comp, pl.ds(row, n), blk(1)] = jnp.where(lane < MARGIN, rolled[0], rolled[1])
        cur[comp, pl.ds(row, n), blk(2)] = jnp.where(
            lane < MARGIN, rolled[1], jnp.where(lane < 80, rolled[2], 0.0))

    def place_rows(ref, n, first):
        @pl.loop(0, n // 16)
        def _(i):
            at = pl.multiple_of(i * 16, 16)
            for comp in (0, 1):
                values = [ref[comp, pl.ds(at, 16), blk(0)], ref[comp, pl.ds(at, 16), blk(1)],
                          jnp.concatenate([ref[comp, pl.ds(at, 16), pl.ds(256, 32)], jnp.zeros((16, 96), F32)], 1)]
                place(comp, first + at, values)

    place_rows(ob, CORE, MARGIN)

    def halo_col_pack(row, at, n):
        lane = lane_iota(n)
        rows = pl.ds(row, n)
        col_s[0, pl.ds(at, n), :] = jnp.where(
            lane < 64, pltpu.roll(cur[0, rows, blk(0)], HALF - 48, 1), pltpu.roll(cur[1, rows, blk(0)], 16, 1))
        col_s[1, pl.ds(at, n), :] = jnp.where(
            lane < 64, pltpu.roll(cur[0, rows, blk(2)], HALF - 32, 1), pltpu.roll(cur[1, rows, blk(2)], 32, 1))

    def halo_col_unpack(side, row, at, n):
        lane = lane_iota(n)
        rows = pl.ds(row, n)
        strip = col_in[side, pl.ds(at, n), :]
        if side == 0:
            for comp, shift in ((0, 0), (1, 64)):
                new = strip if shift == 0 else pltpu.roll(strip, shift, 1)
                cur[comp, rows, blk(0)] = jnp.where(lane < 48, new, cur[comp, rows, blk(0)])
        else:
            for comp, shift in ((0, 80), (1, 16)):
                cur[comp, rows, blk(2)] = jnp.where(lane >= 80, pltpu.roll(strip, shift, 1), cur[comp, rows, blk(2)])

    def col_part(side, part):
        at, n = ((0, CORE), (CORE, 2 * MARGIN))[part]
        return col_s.at[side, pl.ds(at, n), :], col_in.at[1 - side, pl.ds(at, n), :]

    def col_part_in(side, part):
        at, n = ((0, CORE), (CORE, 2 * MARGIN))[part]
        return col_s.at[1 - side, pl.ds(at, n), :], col_in.at[side, pl.ds(at, n), :]

    @pl.loop(0, CORE // 16)
    def _(i):
        halo_col_pack(MARGIN + pl.multiple_of(i * 16, 16), pl.multiple_of(i * 16, 16), 16)

    for side in (0, 1):
        send("col", side, 1, *col_part(side, 0))

    loads[1].wait()
    loads[2].wait()
    for copy in loads[3:]:
        copy.wait()
    live_count = cnt[0, 0]

    @pl.loop(0, SLOTS)
    def _(s):
        r, c = off[0, 0, s, 0], off[0, 0, s, 1]
        live = jnp.where(s < live_count, 1.0, 0.0).astype(F32)
        for comp in (0, 1):
            pr[s, comp] = pltpu.roll(pltpu.roll(pb[comp], r, 0), c, 1) * live
        ap[s] = mm(mm(sv[...], ab[0, 0, s]).astype(BF16), sv[...]).astype(BF16)

    def cols_fix(plain, other, lane):
        return jnp.where(lane == 0, other, plain)

    def forward_rows(s, ranges, total, xbuf):
        r, c = off[0, 0, s, 0], off[0, 0, s, 1]
        at = 0
        for m in chunks(ranges, 16):
            lane = lane_iota(16)
            hi_c = lane < c
            patch = []
            for comp in (0, 1):
                if m < HALF:
                    hi_r = row_iota(16, m) < r
                    three = [
                        jnp.where(hi_r, cur[comp, pl.ds(m + SIDE, 16), blk(b)], cur[comp, pl.ds(m, 16), blk(b)])
                        for b in range(3)
                    ]
                else:
                    three = [cur[comp, pl.ds(m, 16), blk(b)] for b in range(3)]
                patch.append((jnp.where(hi_c, three[2], three[0]), three[1]))
            for b in (0, 1):
                p0, p1 = pr[s, 0, pl.ds(m, 16), blk(b)], pr[s, 1, pl.ds(m, 16), blk(b)]
                xbuf[pl.ds(at, 16), blk(b)] = (p0 * patch[0][b] - p1 * patch[1][b]).astype(BF16)
                xbuf[pl.ds(total + at, 16), blk(b)] = (p0 * patch[1][b] + p1 * patch[0][b]).astype(BF16)
            at += 16
        v = mm(xbuf[...], ttv[...])
        at = 0
        lane = lane_iota(16)
        for m in chunks(ranges, 16):
            c_r, s_r = v[at : at + 16, :HALF], v[at : at + 16, HALF:]
            c_i, s_i = v[total + at : total + at + 16, :HALF], v[total + at : total + at + 16, HALF:]
            hb[s, pl.ds(m, 16), blk(0)] = cols_fix(c_r + s_i, c_r, lane).astype(BF16)
            hb[s, pl.ds(m, 16), blk(1)] = cols_fix(c_r - s_i, s_r, lane).astype(BF16)
            hb[s, pl.ds(m, 16), blk(2)] = cols_fix(c_i - s_r, c_i, lane).astype(BF16)
            hb[s, pl.ds(m, 16), blk(3)] = cols_fix(c_i + s_r, s_i, lane).astype(BF16)
            at += 16

    q_row = {}
    at = 0
    for m in chunks(EDGE, 16):
        q_row[m] = (at, N_EDGE + at)
        at += 16
    at = 2 * N_EDGE
    for m in chunks(INNER, 16):
        q_row[m] = (at, N_INNER + at)
        at += 16

    def middle(s):
        u = mm(tv[...], hb[s])
        lane = lane_iota(16)
        for k in range(0, HALF, 16):
            for b in (0, 1):
                lo, hi = slice(k, k + 16), slice(HALF + k, HALF + k + 16)
                re, im = slice(b * HALF, b * HALF + HALF), slice(SIDE + b * HALF, SIDE + b * HALF + HALF)
                c_r, s_r, c_i, s_i = u[lo, re], u[hi, re], u[lo, im], u[hi, im]
                p_r, p_i, m_r, m_i = c_r + s_i, c_i - s_r, c_r - s_i, c_i + s_r
                if k == 0:
                    first = row_iota(16, 0) == 0
                    p_r, p_i = jnp.where(first, c_r, p_r), jnp.where(first, c_i, p_i)
                    m_r, m_i = jnp.where(first, s_r, m_r), jnp.where(first, s_i, m_i)
                f_p = ap[s, pl.ds(k, 16), blk(b)].astype(F32) * lax.rsqrt(p_r * p_r + p_i * p_i + FLOOR) - 1.0
                f_m = ap[s, pl.ds(HALF + k, 16), blk(b)].astype(F32) * lax.rsqrt(m_r * m_r + m_i * m_i + FLOOR) - 1.0
                p_r, p_i, m_r, m_i = p_r * f_p, p_i * f_p, m_r * f_m, m_i * f_m
                a_r, a_i, nb_i, b_r = p_r + m_r, p_i + m_i, m_i - p_i, p_r - m_r
                if k == 0:
                    a_r, a_i = jnp.where(first, p_r, a_r), jnp.where(first, p_i, a_i)
                    nb_i, b_r = jnp.where(first, m_r, nb_i), jnp.where(first, m_i, b_r)
                wb[pl.ds(k, 16), blk(b)] = a_r.astype(BF16)
                wb[pl.ds(k, 16), blk(2 + b)] = a_i.astype(BF16)
                wb[pl.ds(HALF + k, 16), blk(b)] = nb_i.astype(BF16)
                wb[pl.ds(HALF + k, 16), blk(2 + b)] = b_r.astype(BF16)
        y = mm(ttv[...], wb[...])
        for m in range(0, SIDE, 16):
            rows = slice(m, m + 16)
            p_r, m_r, p_i, m_i = (y[rows, b * HALF : b * HALF + HALF] for b in range(4))
            re, im = q_row[m]
            qb[s, pl.ds(re, 16), blk(0)] = cols_fix(p_r + m_r, p_r, lane).astype(BF16)
            qb[s, pl.ds(re, 16), blk(1)] = cols_fix(m_i - p_i, m_r, lane).astype(BF16)
            qb[s, pl.ds(im, 16), blk(0)] = cols_fix(p_i + m_i, p_i, lane).astype(BF16)
            qb[s, pl.ds(im, 16), blk(1)] = cols_fix(p_r - m_r, m_i, lane).astype(BF16)

    def backward_rows(s, ranges, total, q_at):
        r, c = off[0, 0, s, 0], off[0, 0, s, 1]
        v = mm(qb[s, pl.ds(q_at, 2 * total), :], tv[...])
        at = 0
        for m in chunks(ranges, 16):
            hi_c = lane_iota(16) < c
            terms = ([], [])
            for b in (0, 1):
                b_r = v[at : at + 16, b * HALF : b * HALF + HALF]
                b_i = v[total + at : total + at + 16, b * HALF : b * HALF + HALF]
                p0, p1 = pr[s, 0, pl.ds(m, 16), blk(b)], pr[s, 1, pl.ds(m, 16), blk(b)]
                terms[0].append(p0 * b_r + p1 * b_i)
                terms[1].append(p0 * b_i - p1 * b_r)
            for comp in (0, 1):
                high = jnp.where(hi_c, terms[comp][0], 0.0)
                three = (terms[comp][0] - high, terms[comp][1], high)
                for b in range(3):
                    if m < HALF:
                        below = jnp.where(row_iota(16, m) < r, three[b], 0.0)
                        g[comp, pl.ds(m, 16), blk(b)] += three[b] - below
                        g[comp, pl.ds(m + SIDE, 16), blk(b)] += below
                    else:
                        g[comp, pl.ds(m, 16), blk(b)] += three[b]
            at += 16

    def zero_gradient():
        @pl.loop(0, TILE // 16)
        def _(i):
            for comp in (0, 1):
                g[comp, pl.ds(pl.multiple_of(i * 16, 16), 16), :] = jnp.zeros((16, TILE), F32)

    def each_slot(f):
        @pl.loop(0, SLOTS)
        def _(s):
            f(s)

    for side in (0, 1):
        arrived("col", side, 1, *col_part_in(side, 0))

        @pl.when(has["col", side])
        def _(side=side):
            @pl.loop(0, CORE // 16)
            def _(i):
                halo_col_unpack(side, MARGIN + pl.multiple_of(i * 16, 16), pl.multiple_of(i * 16, 16), 16)

    zero_gradient()
    each_slot(lambda s: forward_rows(s, INNER, N_INNER, xi))

    for side in (0, 1):
        first = 0 if side == 0 else TILE - MARGIN
        arrived("row", side, 0, ob.at[:, pl.ds(0, MARGIN), :], row_in.at[side])

        @pl.when(has["row", side])
        def _(side=side, first=first):
            place_rows(row_in.at[side], MARGIN, first)

        @pl.when(jnp.logical_not(has["row", side]))
        def _(first=first):
            for comp in (0, 1):
                cur[comp, pl.ds(first, MARGIN), :] = jnp.zeros((MARGIN, TILE), F32)

        for j in range(0, MARGIN, 16):
            halo_col_pack(first + j, CORE + side * MARGIN + j, 16)
    for side in (0, 1):
        send("col", side, 2, *col_part(side, 1))
    for side in (0, 1):
        arrived("col", side, 2, *col_part_in(side, 1))

        @pl.when(has["col", side])
        def _(side=side):
            for part in (0, 1):
                for j in range(0, MARGIN, 16):
                    halo_col_unpack(side, (0, TILE - MARGIN)[part] + j, CORE + part * MARGIN + j, 16)

    each_slot(lambda s: forward_rows(s, EDGE, N_EDGE, xe))
    each_slot(middle)
    each_slot(lambda s: backward_rows(s, EDGE, N_EDGE, 0))

    WIDE = 2 * MARGIN

    def stage(dst, src_row, n_rows):
        for comp in (0, 1):
            for j in range(0, n_rows, 16):
                dst[comp, pl.ds(j, 16), :] = g[comp, pl.ds(src_row + j, 16), :]

    each_slot(lambda s: backward_rows(s, INNER, N_INNER, 2 * N_EDGE))

    for side in (0, 1):
        stage(grow_s.at[side], 0 if side == 0 else TILE - WIDE, WIDE)
    for side in (0, 1):
        send("row", side, 3, grow_s.at[side], grow_in.at[1 - side])

    def gcol_rows(part):
        return ((WIDE, 192),) if part == 0 else ((0, WIDE), (TILE - WIDE, WIDE))

    def gcol_index(part):
        first, second = (WIDE, 2 * WIDE) if part == 0 else (0, TILE - WIDE)
        return [(first + j, second + j, j) for j in range(0, WIDE, 16)]

    def gcol_pack(part):
        lane = lane_iota(16)
        base = part * 288
        for row_a, row_b, j in gcol_index(part):
            for side in (0, 1):
                kept = []
                for row, at in ((row_a, j), (row_b, WIDE + j)):
                    re = g[0, pl.ds(row, 16), blk(0 if side == 0 else 2)]
                    im = g[1, pl.ds(row, 16), blk(0 if side == 0 else 2)]
                    if side == 1:
                        re, im = pltpu.roll(re, 96, 1), pltpu.roll(im, 96, 1)
                    gcol_s[side, pl.ds(base + at, 16), :] = jnp.where(lane < 96, re, pltpu.roll(im, 96, 1))
                    kept.append(im)
                gcol_s[side, pl.ds(base + 192 + j, 16), :] = jnp.where(
                    lane < 64, pltpu.roll(kept[0], 96, 1), pltpu.roll(kept[1], 32, 1))

    def gcol_unpack(side, part):
        lane = lane_iota(16)
        base = part * 288
        b = 0 if side == 0 else 2
        for row_a, row_b, j in gcol_index(part):
            rest = gcol_in[side, pl.ds(base + 192 + j, 16), :]
            for row, at, shift in ((row_a, j, 32), (row_b, WIDE + j, 96)):
                strip = gcol_in[side, pl.ds(base + at, 16), :]
                re = jnp.where(lane < 96, strip, 0.0)
                im = jnp.where(lane < 32, pltpu.roll(strip, 32, 1), pltpu.roll(rest, shift, 1))
                im = jnp.where(lane < 96, im, 0.0)
                if side == 1:
                    re, im = pltpu.roll(re, 32, 1), pltpu.roll(im, 32, 1)
                g[0, pl.ds(row, 16), blk(b)] += re
                g[1, pl.ds(row, 16), blk(b)] += im

    def gcol_part(side, part):
        rows = pl.ds(part * 288, 288)
        return gcol_s.at[side, rows, :], gcol_in.at[1 - side, rows, :]

    def gcol_part_in(side, part):
        rows = pl.ds(part * 288, 288)
        return gcol_s.at[1 - side, rows, :], gcol_in.at[side, rows, :]

    gcol_pack(0)
    for side in (0, 1):
        send("col", side, 4, *gcol_part(side, 0))
    for side in (0, 1):
        arrived("row", side, 3, grow_s.at[1 - side], grow_in.at[side])

        @pl.when(has["row", side])
        def _(side=side):
            first = 0 if side == 0 else TILE - WIDE
            for comp in (0, 1):
                for j in range(0, WIDE, 16):
                    g[comp, pl.ds(first + j, 16), :] += grow_in[side, comp, pl.ds(j, 16), :]
    gcol_pack(1)
    for side in (0, 1):
        send("col", side, 5, *gcol_part(side, 1))
    for part in (0, 1):
        for side in (0, 1):
            arrived("col", side, 4 + part, *gcol_part_in(side, part))

            @pl.when(has["col", side])
            def _(side=side, part=part):
                gcol_unpack(side, part)

    @pl.loop(0, TILE // 16)
    def _(i):
        at = pl.multiple_of(i * 16, 16)
        lane, row = lane_iota(16), row_iota(16, at)
        keep = [None] * 3
        row_ok = jnp.logical_and(jnp.logical_or(row >= MARGIN, has["row", 0]),
                                 jnp.logical_or(row < TILE - MARGIN, has["row", 1]))
        keep[0] = jnp.logical_and(row_ok, jnp.logical_or(lane >= MARGIN, has["col", 0]))
        keep[1] = row_ok
        keep[2] = jnp.logical_and(row_ok, jnp.logical_or(lane < 80, has["col", 1]))
        for comp in (0, 1):
            for b in range(3):
                cur[comp, pl.ds(at, 16), blk(b)] += jnp.where(
                    keep[b], STEP * g[comp, pl.ds(at, 16), blk(b)], 0.0)

    zero_gradient()
    each_slot(lambda s: forward_rows(s, INNER, N_INNER, xi))
    each_slot(lambda s: forward_rows(s, EDGE, N_EDGE, xe))
    each_slot(middle)
    each_slot(lambda s: backward_rows(s, EDGE, N_EDGE, 0))

    for side in (0, 1):
        first = 0 if side == 0 else TILE - MARGIN
        stage(frow_s.at[side], first, MARGIN)
    for side in (0, 1):
        send("row", side, 6, frow_s.at[side], frow_in.at[1 - side])
    each_slot(lambda s: backward_rows(s, INNER, N_INNER, 2 * N_EDGE))

    def fcol_index(part):
        if part == 0:
            return [(2 * MARGIN + j, j) for j in range(0, 192, 16)]
        return [(MARGIN + j, 192 + j) for j in range(0, MARGIN, 16)] + [
            (TILE - 2 * MARGIN + j, 240 + j) for j in range(0, MARGIN, 16)]

    def fcol_pack(part):
        lane = lane_iota(16)
        for row, at in fcol_index(part):
            rows, to_rows = pl.ds(row, 16), pl.ds(at, 16)
            fcol_s[0, to_rows, :] = jnp.where(
                lane < 64, g[0, rows, blk(0)], pltpu.roll(g[1, rows, blk(0)], 64, 1))
            fcol_s[1, to_rows, :] = jnp.where(
                lane < 64, pltpu.roll(g[0, rows, blk(2)], 48, 1), pltpu.roll(g[1, rows, blk(2)], 112, 1))

    def fcol_unpack(side, part):
        lane = lane_iota(16)
        for row, at in fcol_index(part):
            strip = fcol_in[side, pl.ds(at, 16), :]
            if side == 0:
                b, ok = 0, jnp.logical_and(lane >= 48, lane < 96)
                pair = (pltpu.roll(strip, 48, 1), pltpu.roll(strip, 112, 1))
            else:
                b, ok = 2, jnp.logical_and(lane >= 32, lane < 80)
                pair = (pltpu.roll(strip, 32, 1), pltpu.roll(strip, 96, 1))
            for comp in (0, 1):
                g[comp, pl.ds(row, 16), blk(b)] += jnp.where(ok, pair[comp], 0.0)

    def fcol_part(side, part):
        rows = pl.ds(*((0, 192), (192, 96))[part])
        return fcol_s.at[side, rows, :], fcol_in.at[1 - side, rows, :]

    def fcol_part_in(side, part):
        rows = pl.ds(*((0, 192), (192, 96))[part])
        return fcol_s.at[1 - side, rows, :], fcol_in.at[side, rows, :]

    fcol_pack(0)
    for side in (0, 1):
        send("col", side, 7, *fcol_part(side, 0))
    for side in (0, 1):
        arrived("row", side, 6, frow_s.at[1 - side], frow_in.at[side])

        @pl.when(has["row", side])
        def _(side=side):
            first = MARGIN if side == 0 else TILE - 2 * MARGIN
            for comp in (0, 1):
                for j in range(0, MARGIN, 16):
                    g[comp, pl.ds(first + j, 16), :] += frow_in[side, comp, pl.ds(j, 16), :]
    fcol_pack(1)
    for side in (0, 1):
        send("col", side, 8, *fcol_part(side, 1))
    for part in (0, 1):
        for side in (0, 1):
            arrived("col", side, 7 + part, *fcol_part_in(side, part))

            @pl.when(has["col", side])
            def _(side=side, part=part):
                fcol_unpack(side, part)

    @pl.loop(0, CORE // 16)
    def _(i):
        at = pl.multiple_of(i * 16, 16)
        lane = lane_iota(16)
        for comp in (0, 1):
            v = [
                pltpu.roll(cur[comp, pl.ds(MARGIN + at, 16), blk(b)] + STEP * g[comp, pl.ds(MARGIN + at, 16), blk(b)],
                           80, 1)
                for b in range(3)
            ]
            out[comp, pl.ds(at, 16), blk(0)] = jnp.where(lane < 80, v[0], v[1])
            out[comp, pl.ds(at, 16), blk(1)] = jnp.where(lane < 80, v[1], v[2])
            out[comp, pl.ds(at, 16), pl.ds(256, 32)] = v[2][:, :32]

    for side in (0, 1):
        sent("row", side, 0, *halo_row(side))
        sent("col", side, 1, *col_part(side, 0))
        sent("col", side, 2, *col_part(side, 1))
        sent("row", side, 3, grow_s.at[side], grow_in.at[1 - side])
        sent("col", side, 4, *gcol_part(side, 0))
        sent("col", side, 5, *gcol_part(side, 1))
        sent("row", side, 6, frow_s.at[side], frow_in.at[1 - side])
        sent("col", side, 7, *fcol_part(side, 0))
        sent("col", side, 8, *fcol_part(side, 1))


def shards(object_field, probe, amplitudes, offsets, counts):
    table, table_t, swap = (jnp.asarray(a) for a in half_tables())
    anywhere = pl.BlockSpec(memory_space=pl.ANY)
    scalars = pl.BlockSpec(memory_space=pltpu.SMEM)
    v32 = lambda *shape: pltpu.VMEM(shape, F32)
    v16 = lambda *shape: pltpu.VMEM(shape, BF16)
    return pl.pallas_call(
        kernel,
        out_shape=jax.ShapeDtypeStruct(object_field.shape, F32),
        in_specs=[scalars, scalars] + [anywhere] * 6,
        out_specs=pl.BlockSpec(memory_space=pltpu.VMEM),
        scratch_shapes=[
            v32(2, CORE, CORE), v32(2, SIDE, SIDE), v16(1, 1, SLOTS, SIDE, SIDE),
            v16(SIDE, SIDE), v16(SIDE, SIDE), v16(SIDE, SIDE),
            v32(SLOTS, 2, SIDE, SIDE), v16(SLOTS, SIDE, SIDE),
            v16(SLOTS, SIDE, 2 * SIDE), v16(SIDE, 2 * SIDE), v16(SLOTS, 2 * SIDE, SIDE),
            v16(2 * N_EDGE, SIDE), v16(2 * N_INNER, SIDE),
            v32(2, TILE, TILE), v32(2, TILE, TILE),
            v32(2, 2, MARGIN, CORE), v32(2, TILE, HALF), v32(2, TILE, HALF),
            v32(2, 2, 2 * MARGIN, TILE), v32(2, 2, 2 * MARGIN, TILE),
            v32(2, 576, HALF), v32(2, 576, HALF),
            v32(2, 2, MARGIN, TILE), v32(2, 2, MARGIN, TILE),
            v32(2, CORE, HALF), v32(2, CORE, HALF),
            pltpu.SemaphoreType.DMA((6,)),
            pltpu.SemaphoreType.DMA((18,)),
            pltpu.SemaphoreType.DMA((18,)),
        ],
        compiler_params=pltpu.CompilerParams(
            collective_id=0, has_side_effects=True, vmem_limit_bytes=60 * 1024 * 1024),
        name="ptycho",
    )(offsets, counts, object_field, probe, amplitudes, table, table_t, swap)


def solution(mesh):
    return jax.shard_map(
        shards,
        mesh=mesh,
        in_specs=(
            P(None, "row", "col"),
            P(),
            P("row", "col", None, None, None),
            P("row", "col", None, None),
            P("row", "col"),
        ),
        out_specs=P(None, "row", "col"),
        check_vma=False,
    )
```

time: 470 us -> 86.5 us (0.18)
  the two profiles are of different devices: /device:TPU:14 before, /device:TPU:45 now
where the time goes in v1:
time: 86.5 us; the launch traced here: 86.3 us
  Pallas kernels  82.8 us (96%)
  local copies, waits for them, and re-layouts  2.82 us (3%)
    pallas_call x1, Pallas kernels, shards(): pl.pallas_call(kernel, out_shape=jax.ShapeDtypeStruct(object_field.shape,...  82.8 us
    unnamed x4, local copies, waits for them, and re-layouts  2.82 us

profile of v1, /device:TPU:45, one launch (start us, length us, event | category | flops | bytes accessed | tf_op | source)
XLA Modules:
  0.0 86.3 jit_solution(194470945308927703)
XLA Ops:
  0.0 0.0 copy-start
  0.7 0.0 copy-done
  0.7 0.7 copy.9.off
  1.4 82.8 %ptycho.1 = f32[2,288,288]{2,1,0:T(8,128)} custom-call(s32[1,1,8,2]{3,2,1,0:T(8,128)} %copy.9.off, s32[1,1]{1,0:T(1,128)S(6)} %copy.11.cnt, f32[2,288,288]{2,1,0:T(8,128)} %obj.1, f32[2,256,256]{2,1,0:T(8,128)} %probe.1, bf16[1,1,8,256,256]{4,3,2,1,0:T(8,128)(2,1)} %amp.1, bf16[256,256]{1,0:T(8,128)(2,1)} %constant.6.clone.table, ...), custom_call_target="tpu_custom_call" | custom-call | tf_op jit(solution)/shard_map/ptycho/pallas_call | solution.py:564
  84.2 2.1 %copy.12 = f32[2,288,288]{2,1,0:T(8,128)} copy(f32[2,288,288]{2,1,0:T(8,128)} %ptycho.1) | data formatting | bytes 1327104
Async XLA Ops:
  0.0 0.7 copy-start

commit v2 on v1

v2 whole, which is shorter than its diff:
```python
import functools
import math

import jax
import jax.numpy as jnp
import numpy as np
from jax import lax
from jax.experimental import pallas as pl
from jax.experimental.pallas import tpu as pltpu
from jax.sharding import PartitionSpec as P

MARGIN = 48
PASSES = 2
SIDE = 256
HALF = 128
CORE = 288
TILE = 384
SLOTS = 8
STEP = 0.1
FLOOR = 0.01
F32 = jnp.float32
BF16 = jnp.bfloat16

WIDE = 2 * MARGIN

EDGE, INNER = 0, HALF


def half_tables():
    position = np.arange(SIDE)
    angle = (position[:, None] * position[None, :] % SIDE) * (2.0 * math.pi / SIDE)
    scale = 1.0 / math.sqrt(SIDE)
    cosine, sine = np.cos(angle) * scale, np.sin(angle) * scale
    table = np.concatenate([cosine[:HALF], cosine[HALF : HALF + 1], sine[1:HALF]])
    order = np.concatenate([np.arange(HALF), [HALF], np.arange(SIDE - 1, HALF, -1)])
    swap = np.zeros((SIDE, SIDE), np.float32)
    swap[np.arange(SIDE), order] = 1.0
    return [a.astype(jnp.bfloat16) for a in (table, table.T, swap)]


def mm(a, b):
    return jnp.dot(a, b, preferred_element_type=F32)


def lane_iota(rows):
    return lax.broadcasted_iota(jnp.int32, (rows, HALF), 1)


def row_iota(rows, start):
    return lax.broadcasted_iota(jnp.int32, (rows, HALF), 0) + start


def blk(n):
    return pl.ds(n * HALF, HALF)


def kernel(
    off, cnt, obj, probe, amp, table, table_t, swap, out,
    ob, pb, ab, tv, ttv, sv,
    pr, ap, hb, wb, qb, xb, cur, ga, gb,
    row_in, col_s, col_in, grow_s, grow_in, gcol_s, gcol_in, frow_s, frow_in, fcol_s, fcol_in,
    load_sem, send_sem, recv_sem,
):
    n_row, n_col = lax.axis_size("row"), lax.axis_size("col")
    me_r, me_c = lax.axis_index("row"), lax.axis_index("col")
    has = {("row", 0): me_r > 0, ("row", 1): me_r < n_row - 1, ("col", 0): me_c > 0, ("col", 1): me_c < n_col - 1}
    to = {("row", 0): me_r - 1, ("row", 1): me_r + 1, ("col", 0): me_c - 1, ("col", 1): me_c + 1}
    sides = [(axis, side) for axis in ("row", "col") for side in (0, 1)]
    corners = [(a, b) for a in (0, 1) for b in (0, 1)]

    def peer(key):
        if key in has:
            return has[key], {key[0]: to[key]}
        rows, cols = ("row", key[0]), ("col", key[1])
        return jnp.logical_and(has[rows], has[cols]), {"row": to[rows], "col": to[cols]}

    def other(key):
        return (key[0], 1 - key[1]) if key in has else (1 - key[0], 1 - key[1])

    loads = [
        pltpu.make_async_copy(src, dst, load_sem.at[i])
        for i, (src, dst) in enumerate(
            ((obj, ob), (probe, pb), (amp, ab), (table, tv), (table_t, ttv), (swap, sv))
        )
    ]
    for copy in loads:
        copy.start()

    barrier = pltpu.get_barrier_semaphore()
    for key in sides + corners:
        ok, device = peer(key)

        @pl.when(ok)
        def _(device=device):
            pl.semaphore_signal(barrier, inc=1, device_id=device, device_id_type=pl.DeviceIdType.MESH)
    pl.semaphore_wait(barrier, sum(peer(key)[0].astype(jnp.int32) for key in sides + corners))

    kinds, started = {}, []

    def semaphore(kind, key):
        return kinds.setdefault((kind, key), len(kinds))

    def remote(key, kind, src, dst, outgoing):
        here, there = (key, other(key)) if outgoing else (other(key), key)
        return pltpu.make_async_remote_copy(
            src_ref=src, dst_ref=dst,
            send_sem=send_sem.at[semaphore(kind, here)],
            recv_sem=recv_sem.at[semaphore(kind, there)],
            device_id=peer(key)[1],
            device_id_type=pl.DeviceIdType.MESH,
        )

    def send(key, kind, src, dst):
        started.append((key, kind, src, dst))

        @pl.when(peer(key)[0])
        def _():
            remote(key, kind, src, dst, True).start()

    def arrived(key, kind, src, dst):
        @pl.when(peer(key)[0])
        def _():
            remote(key, kind, src, dst, False).wait_recv()

    loads[0].wait()
    for side in (0, 1):
        start = 0 if side == 0 else CORE - MARGIN
        send(("row", side), 0, ob.at[:, pl.ds(start, MARGIN), :], row_in.at[1 - side])

    def halo_col_pack(row, n):
        lane, rows = lane_iota(n), pl.ds(row, n)
        re, im = ([ob[comp, rows, blk(0)], ob[comp, rows, blk(1)], ob[comp, rows, pl.ds(256, 32)]] for comp in (0, 1))
        zero = jnp.zeros((n, 96), F32)
        col_s[0, rows, :] = jnp.where(lane < 64, re[0], pltpu.roll(im[0], 64, 1))
        tail = [jnp.where(lane < 32, jnp.concatenate([v[2], zero], 1), v[1]) for v in (re, im)]
        col_s[1, rows, :] = jnp.where(lane < 64, pltpu.roll(tail[0], 16, 1), pltpu.roll(tail[1], 80, 1))

    for row in (0, CORE - MARGIN):
        halo_col_pack(row, MARGIN)
    for a, b in corners:
        send((a, b), 1, col_s.at[b, pl.ds(0 if a == 0 else CORE - MARGIN, MARGIN), :],
             col_in.at[1 - b, pl.ds(CORE + (1 - a) * MARGIN, MARGIN), :])

    @pl.loop(1, CORE // MARGIN - 1)
    def _(i):
        halo_col_pack(pl.multiple_of(i * MARGIN, MARGIN), MARGIN)

    for side in (0, 1):
        send(("col", side), 2, col_s.at[side, :, :], col_in.at[1 - side, pl.ds(0, CORE), :])

    def place_rows(ref, n, first):
        @pl.loop(0, n // MARGIN)
        def _(i):
            at = pl.multiple_of(i * MARGIN, MARGIN)
            rows, to_rows = pl.ds(at, MARGIN), pl.ds(first + at, MARGIN)
            lane = lane_iota(MARGIN)
            for comp in (0, 1):
                a, b = (pltpu.roll(ref[comp, rows, blk(k)], MARGIN, 1) for k in (0, 1))
                c = pltpu.roll(
                    jnp.concatenate([ref[comp, rows, pl.ds(256, 32)], jnp.zeros((MARGIN, 96), F32)], 1), MARGIN, 1)
                cur[comp, to_rows, blk(0)] = jnp.where(lane < MARGIN, 0.0, a)
                cur[comp, to_rows, blk(1)] = jnp.where(lane < MARGIN, a, b)
                cur[comp, to_rows, blk(2)] = jnp.where(lane < MARGIN, b, c)

    place_rows(ob, CORE, MARGIN)

    def halo_col_unpack(side, row, at, n):
        lane, rows = lane_iota(n), pl.ds(row, n)
        strip = col_in[side, pl.ds(at, n), :]
        if side == 0:
            for comp, shift in ((0, 0), (1, 64)):
                new = strip if shift == 0 else pltpu.roll(strip, shift, 1)
                cur[comp, rows, blk(0)] = jnp.where(lane < 48, new, cur[comp, rows, blk(0)])
        else:
            for comp, shift in ((0, 80), (1, 16)):
                cur[comp, rows, blk(2)] = jnp.where(lane >= 80, pltpu.roll(strip, shift, 1), cur[comp, rows, blk(2)])

    @pl.loop(0, TILE // MARGIN)
    def _(i):
        for ref in (ga, gb):
            for comp in (0, 1):
                ref[comp, pl.ds(pl.multiple_of(i * MARGIN, MARGIN), MARGIN), :] = jnp.zeros((MARGIN, TILE), F32)

    loads[1].wait()
    loads[2].wait()
    for copy in loads[3:]:
        copy.wait()
    live_count = cnt[0, 0]

    @pl.loop(0, SLOTS)
    def _(s):
        r, c = off[0, 0, 0, s], off[0, 0, 1, s]
        live = jnp.where(s < live_count, 1.0, 0.0).astype(F32)
        for comp in (0, 1):
            pr[s, comp] = pltpu.roll(pltpu.roll(pb[comp], r, 0), c, 1) * live
        ap[s] = mm(mm(sv[...], ab[0, 0, s]).astype(BF16), sv[...]).astype(BF16)

    def cols_fix(plain, other, lane):
        return jnp.where(lane == 0, other, plain)

    def forward_rows(s, first, buf):
        r, c = off[0, 0, 0, s], off[0, 0, 1, s]
        lane = lane_iota(16)
        hi_c = lane < c
        for at in range(0, HALF, 16):
            m = first + at
            patch = []
            for comp in (0, 1):
                if m < HALF:
                    hi_r = row_iota(16, m) < r
                    three = [
                        jnp.where(hi_r, cur[comp, pl.ds(m + SIDE, 16), blk(b)], cur[comp, pl.ds(m, 16), blk(b)])
                        for b in range(3)
                    ]
                else:
                    three = [cur[comp, pl.ds(m, 16), blk(b)] for b in range(3)]
                patch.append((jnp.where(hi_c, three[2], three[0]), three[1]))
            for b in (0, 1):
                p0, p1 = pr[s, 0, pl.ds(m, 16), blk(b)], pr[s, 1, pl.ds(m, 16), blk(b)]
                xb[buf, pl.ds(at, 16), blk(b)] = (p0 * patch[0][b] - p1 * patch[1][b]).astype(BF16)
                xb[buf, pl.ds(HALF + at, 16), blk(b)] = (p0 * patch[1][b] + p1 * patch[0][b]).astype(BF16)
        v = mm(xb[buf], ttv[...])
        for at in range(0, HALF, 16):
            rows = pl.ds(first + at, 16)
            c_r, s_r = v[at : at + 16, :HALF], v[at : at + 16, HALF:]
            c_i, s_i = v[HALF + at : HALF + at + 16, :HALF], v[HALF + at : HALF + at + 16, HALF:]
            hb[s, rows, blk(0)] = cols_fix(c_r + s_i, c_r, lane).astype(BF16)
            hb[s, rows, blk(1)] = cols_fix(c_r - s_i, s_r, lane).astype(BF16)
            hb[s, rows, blk(2)] = cols_fix(c_i - s_r, c_i, lane).astype(BF16)
            hb[s, rows, blk(3)] = cols_fix(c_i + s_r, s_i, lane).astype(BF16)

    def middle(s, buf):
        u = mm(tv[...], hb[s])
        lane = lane_iota(16)
        for k in range(0, HALF, 16):
            for b in (0, 1):
                lo, hi = slice(k, k + 16), slice(HALF + k, HALF + k + 16)
                re, im = slice(b * HALF, b * HALF + HALF), slice(SIDE + b * HALF, SIDE + b * HALF + HALF)
                c_r, s_r, c_i, s_i = u[lo, re], u[hi, re], u[lo, im], u[hi, im]
                p_r, p_i, m_r, m_i = c_r + s_i, c_i - s_r, c_r - s_i, c_i + s_r
                if k == 0:
                    first = row_iota(16, 0) == 0
                    p_r, p_i = jnp.where(first, c_r, p_r), jnp.where(first, c_i, p_i)
                    m_r, m_i = jnp.where(first, s_r, m_r), jnp.where(first, s_i, m_i)
                f_p = ap[s, pl.ds(k, 16), blk(b)].astype(F32) * lax.rsqrt(p_r * p_r + p_i * p_i + FLOOR) - 1.0
                f_m = ap[s, pl.ds(HALF + k, 16), blk(b)].astype(F32) * lax.rsqrt(m_r * m_r + m_i * m_i + FLOOR) - 1.0
                p_r, p_i, m_r, m_i = p_r * f_p, p_i * f_p, m_r * f_m, m_i * f_m
                a_r, a_i, nb_i, b_r = p_r + m_r, p_i + m_i, m_i - p_i, p_r - m_r
                if k == 0:
                    a_r, a_i = jnp.where(first, p_r, a_r), jnp.where(first, p_i, a_i)
                    nb_i, b_r = jnp.where(first, m_r, nb_i), jnp.where(first, m_i, b_r)
                wb[buf, pl.ds(k, 16), blk(b)] = a_r.astype(BF16)
                wb[buf, pl.ds(k, 16), blk(2 + b)] = a_i.astype(BF16)
                wb[buf, pl.ds(HALF + k, 16), blk(b)] = nb_i.astype(BF16)
                wb[buf, pl.ds(HALF + k, 16), blk(2 + b)] = b_r.astype(BF16)
        y = mm(ttv[...], wb[buf])
        for m in range(0, SIDE, 16):
            rows = slice(m, m + 16)
            p_r, m_r, p_i, m_i = (y[rows, b * HALF : b * HALF + HALF] for b in range(4))
            re = m if m < HALF else HALF + m
            im = re + HALF
            qb[s, pl.ds(re, 16), blk(0)] = cols_fix(p_r + m_r, p_r, lane).astype(BF16)
            qb[s, pl.ds(re, 16), blk(1)] = cols_fix(m_i - p_i, m_r, lane).astype(BF16)
            qb[s, pl.ds(im, 16), blk(0)] = cols_fix(p_i + m_i, p_i, lane).astype(BF16)
            qb[s, pl.ds(im, 16), blk(1)] = cols_fix(p_r - m_r, m_i, lane).astype(BF16)

    def backward_rows(s, first, g):
        products = [mm(qb[slot, pl.ds(2 * first, SIDE), :], tv[...]) for slot in s]
        lane = lane_iota(16)
        for at in range(0, HALF, 16):
            m = first + at
            total = [[None] * 3, [None] * 3]
            below = [[None] * 3, [None] * 3]
            for slot, v in zip(s, products):
                r, c = off[0, 0, 0, slot], off[0, 0, 1, slot]
                terms = ([], [])
                for b in (0, 1):
                    b_r = v[at : at + 16, b * HALF : b * HALF + HALF]
                    b_i = v[HALF + at : HALF + at + 16, b * HALF : b * HALF + HALF]
                    p0, p1 = pr[slot, 0, pl.ds(m, 16), blk(b)], pr[slot, 1, pl.ds(m, 16), blk(b)]
                    terms[0].append(p0 * b_r + p1 * b_i)
                    terms[1].append(p0 * b_i - p1 * b_r)
                for comp in (0, 1):
                    left = terms[comp][0]
                    high = jnp.where(lane < c, left, 0.0)
                    for b, value in enumerate((left - high, terms[comp][1], high)):
                        if m < HALF:
                            low = jnp.where(row_iota(16, m) < r, value, 0.0)
                            value = value - low
                            below[comp][b] = low if below[comp][b] is None else below[comp][b] + low
                        total[comp][b] = value if total[comp][b] is None else total[comp][b] + value
            for comp in (0, 1):
                for b in range(3):
                    g[comp, pl.ds(m, 16), blk(b)] += total[comp][b]
                    if m < HALF:
                        g[comp, pl.ds(m + SIDE, 16), blk(b)] += below[comp][b]

    def forward(first):
        @pl.loop(0, SLOTS // 2)
        def _(i):
            for buf in (0, 1):
                forward_rows(2 * i + buf, first, buf)

    def middles():
        @pl.loop(0, SLOTS // 2)
        def _(i):
            for buf in (0, 1):
                middle(2 * i + buf, buf)

    def backward(first, g):
        @pl.loop(0, SLOTS // 2)
        def _(i):
            backward_rows((2 * i, 2 * i + 1), first, g)

    for side in (0, 1):
        arrived(("col", side), 2, col_s.at[1 - side, :, :], col_in.at[side, pl.ds(0, CORE), :])

        @pl.when(has["col", side])
        def _(side=side):
            @pl.loop(0, CORE // MARGIN)
            def _(i):
                at = pl.multiple_of(i * MARGIN, MARGIN)
                halo_col_unpack(side, MARGIN + at, at, MARGIN)

    forward(INNER)

    for side in (0, 1):
        first = 0 if side == 0 else TILE - MARGIN
        arrived(("row", side), 0, ob.at[:, pl.ds(0, MARGIN), :], row_in.at[side])

        @pl.when(has["row", side])
        def _(side=side, first=first):
            place_rows(row_in.at[side], MARGIN, first)

        @pl.when(jnp.logical_not(has["row", side]))
        def _(first=first):
            for comp in (0, 1):
                cur[comp, pl.ds(first, MARGIN), :] = jnp.zeros((MARGIN, TILE), F32)
    for a, b in corners:
        at = CORE + a * MARGIN
        arrived((a, b), 1, col_s.at[1 - b, pl.ds(0, MARGIN), :], col_in.at[b, pl.ds(at, MARGIN), :])

        @pl.when(peer((a, b))[0])
        def _(a=a, b=b, at=at):
            halo_col_unpack(b, a * (TILE - MARGIN), at, MARGIN)

    forward(EDGE)
    middles()
    backward(EDGE, ga)

    def stage(dst, g, src_row, n_rows):
        for b in range(3):
            for comp in (0, 1):
                dst[b, comp] = g[comp, pl.ds(src_row, n_rows), blk(b)]

    def send_rows(src, dst, kind):
        for side in (0, 1):
            for b in (0, 2):
                send(("row", side), kind + (b,), src.at[side, b], dst.at[1 - side, b])
        for side in (0, 1):
            send(("row", side), kind + (1,), src.at[side, 1], dst.at[1 - side, 1])

    def add_rows(src, dst, kind, g, first, n_rows, blocks):
        for side in (0, 1):
            for b in blocks:
                arrived(("row", side), kind + (b,), src.at[1 - side, b], dst.at[side, b])

            @pl.when(has["row", side])
            def _(side=side):
                for b in blocks:
                    for comp in (0, 1):
                        g[comp, pl.ds(first[side], n_rows), blk(b)] += dst[side, b, comp]

    for side in (0, 1):
        stage(grow_s.at[side], ga, 0 if side == 0 else TILE - WIDE, WIDE)
    send_rows(grow_s, grow_in, ("g",))
    backward(INNER, ga)

    def gcol_index(part):
        first, second = (WIDE, 2 * WIDE) if part == 0 else (0, TILE - WIDE)
        return [(first + j, second + j, j) for j in range(0, WIDE, MARGIN)]

    def gcol_pack(part):
        n = MARGIN
        lane = lane_iota(n)
        base = part * 288
        for row_a, row_b, j in gcol_index(part):
            for side in (0, 1):
                kept = []
                for row, at in ((row_a, j), (row_b, WIDE + j)):
                    re = ga[0, pl.ds(row, n), blk(0 if side == 0 else 2)]
                    im = ga[1, pl.ds(row, n), blk(0 if side == 0 else 2)]
                    if side == 1:
                        strip = jnp.where(lane < 96, pltpu.roll(re, 96, 1), pltpu.roll(im, 64, 1))
                    else:
                        strip = jnp.where(lane < 96, re, pltpu.roll(im, 96, 1))
                    gcol_s[side, pl.ds(base + at, n), :] = strip
                    kept.append(im)
                shift = (96, 32) if side == 0 else (64, 0)
                low = pltpu.roll(kept[0], shift[0], 1)
                high = pltpu.roll(kept[1], shift[1], 1) if shift[1] else kept[1]
                gcol_s[side, pl.ds(base + 192 + j, n), :] = jnp.where(lane < 64, low, high)

    def gcol_unpack(side, part):
        n = MARGIN
        lane = lane_iota(n)
        base = part * 288
        for row_a, row_b, j in gcol_index(part):
            rest = gcol_in[side, pl.ds(base + 192 + j, n), :]
            for row, at, shift in ((row_a, j, 0), (row_b, WIDE + j, 64)):
                strip = gcol_in[side, pl.ds(base + at, n), :]
                if side == 0:
                    re = jnp.where(lane < 96, strip, 0.0)
                    im = jnp.where(lane < 32, pltpu.roll(strip, 32, 1), pltpu.roll(rest, 32 + shift, 1))
                    im = jnp.where(lane < 96, im, 0.0)
                else:
                    re = jnp.where(lane < 32, 0.0, pltpu.roll(strip, 32, 1))
                    tail = pltpu.roll(rest, 64 + shift, 1) if shift == 0 else rest
                    im = jnp.where(lane < 64, pltpu.roll(strip, 64, 1), tail)
                    im = jnp.where(lane < 32, 0.0, im)
                b = 0 if side == 0 else 2
                ga[0, pl.ds(row, n), blk(b)] += re
                ga[1, pl.ds(row, n), blk(b)] += im

    def gcol_send(part):
        rows = pl.ds(part * 288, 288)
        for side in (0, 1):
            send(("col", side), 3 + part, gcol_s.at[side, rows, :], gcol_in.at[1 - side, rows, :])

    def gcol_add(part):
        rows = pl.ds(part * 288, 288)
        for side in (0, 1):
            arrived(("col", side), 3 + part, gcol_s.at[1 - side, rows, :], gcol_in.at[side, rows, :])

            @pl.when(has["col", side])
            def _(side=side):
                gcol_unpack(side, part)

    def update(rows):
        for at in rows:
            lane = lane_iota(MARGIN)
            ok = True
            if at == 0:
                ok = has["row", 0]
            elif at == TILE - MARGIN:
                ok = has["row", 1]
            keep = (
                jnp.logical_and(ok, jnp.logical_or(lane >= MARGIN, has["col", 0])),
                jnp.logical_and(ok, lane >= 0),
                jnp.logical_and(ok, jnp.logical_or(lane < 80, has["col", 1])),
            )
            for comp in (0, 1):
                for b in range(3):
                    cur[comp, pl.ds(at, MARGIN), blk(b)] += jnp.where(
                        keep[b], STEP * ga[comp, pl.ds(at, MARGIN), blk(b)], 0.0)

    gcol_pack(0)
    gcol_send(0)
    gcol_add(0)
    update(range(WIDE, TILE - WIDE, MARGIN))
    forward(INNER)

    first = (0, TILE - WIDE)
    add_rows(grow_s, grow_in, ("g",), ga, first, WIDE, (0, 2))
    gcol_pack(1)
    gcol_send(1)
    add_rows(grow_s, grow_in, ("g",), ga, first, WIDE, (1,))
    gcol_add(1)
    update((0, MARGIN, TILE - WIDE, TILE - MARGIN))

    forward(EDGE)
    middles()
    backward(EDGE, gb)
    for side in (0, 1):
        stage(frow_s.at[side], gb, 0 if side == 0 else TILE - MARGIN, MARGIN)
    send_rows(frow_s, frow_in, ("f",))
    backward(INNER, gb)

    def fcol_index(part):
        if part == 0:
            return [(WIDE + j, j) for j in range(0, 192, MARGIN)]
        return [(MARGIN, 192), (TILE - WIDE, 240)]

    def fcol_pack(part):
        lane = lane_iota(MARGIN)
        for row, at in fcol_index(part):
            rows, to_rows = pl.ds(row, MARGIN), pl.ds(at, MARGIN)
            fcol_s[0, to_rows, :] = jnp.where(
                lane < 64, gb[0, rows, blk(0)], pltpu.roll(gb[1, rows, blk(0)], 64, 1))
            fcol_s[1, to_rows, :] = jnp.where(
                lane < 64, pltpu.roll(gb[0, rows, blk(2)], 48, 1), pltpu.roll(gb[1, rows, blk(2)], 112, 1))

    def fcol_unpack(side, part):
        lane = lane_iota(MARGIN)
        for row, at in fcol_index(part):
            strip = fcol_in[side, pl.ds(at, MARGIN), :]
            if side == 0:
                b, ok = 0, jnp.logical_and(lane >= 48, lane < 96)
                pair = (pltpu.roll(strip, 48, 1), pltpu.roll(strip, 112, 1))
            else:
                b, ok = 2, jnp.logical_and(lane >= 32, lane < 80)
                pair = (pltpu.roll(strip, 32, 1), pltpu.roll(strip, 96, 1))
            for comp in (0, 1):
                gb[comp, pl.ds(row, MARGIN), blk(b)] += jnp.where(ok, pair[comp], 0.0)

    def fcol_send(part):
        rows = pl.ds(*((0, 192), (192, 96))[part])
        for side in (0, 1):
            send(("col", side), 5 + part, fcol_s.at[side, rows, :], fcol_in.at[1 - side, rows, :])

    def fcol_add(part):
        rows = pl.ds(*((0, 192), (192, 96))[part])
        for side in (0, 1):
            arrived(("col", side), 5 + part, fcol_s.at[1 - side, rows, :], fcol_in.at[side, rows, :])

            @pl.when(has["col", side])
            def _(side=side):
                fcol_unpack(side, part)

    def write(row):
        lane, rows, to_rows = lane_iota(MARGIN), pl.ds(row, MARGIN), pl.ds(row - MARGIN, MARGIN)
        for comp in (0, 1):
            v = [pltpu.roll(cur[comp, rows, blk(b)] + STEP * gb[comp, rows, blk(b)], 80, 1) for b in range(3)]
            out[comp, to_rows, blk(0)] = jnp.where(lane < 80, v[0], v[1])
            out[comp, to_rows, blk(1)] = jnp.where(lane < 80, v[1], v[2])
            out[comp, to_rows, pl.ds(256, 32)] = v[2][:, :32]

    fcol_pack(0)
    fcol_send(0)
    fcol_add(0)
    for row in range(WIDE, TILE - WIDE, MARGIN):
        write(row)
    first = (MARGIN, TILE - WIDE)
    add_rows(frow_s, frow_in, ("f",), gb, first, MARGIN, (0, 2))
    fcol_pack(1)
    fcol_send(1)
    add_rows(frow_s, frow_in, ("f",), gb, first, MARGIN, (1,))
    fcol_add(1)
    for row in first:
        write(row)

    for key, kind, src, dst in started:
        @pl.when(peer(key)[0])
        def _(args=(key, kind, src, dst, True)):
            remote(*args).wait_send()


def shards(object_field, probe, amplitudes, offsets, counts):
    table, table_t, swap = (jnp.asarray(a) for a in half_tables())
    anywhere = pl.BlockSpec(memory_space=pl.ANY)
    scalars = pl.BlockSpec(memory_space=pltpu.SMEM)
    v32 = lambda *shape: pltpu.VMEM(shape, F32)
    v16 = lambda *shape: pltpu.VMEM(shape, BF16)
    return pl.pallas_call(
        kernel,
        out_shape=jax.ShapeDtypeStruct(object_field.shape, F32),
        in_specs=[scalars, scalars] + [anywhere] * 6,
        out_specs=pl.BlockSpec(memory_space=pltpu.VMEM),
        scratch_shapes=[
            v32(2, CORE, CORE), v32(2, SIDE, SIDE), v16(1, 1, SLOTS, SIDE, SIDE),
            v16(SIDE, SIDE), v16(SIDE, SIDE), v16(SIDE, SIDE),
            v32(SLOTS, 2, SIDE, SIDE), v16(SLOTS, SIDE, SIDE),
            v16(SLOTS, SIDE, 2 * SIDE), v16(2, SIDE, 2 * SIDE), v16(SLOTS, 2 * SIDE, SIDE), v16(2, SIDE, SIDE),
            v32(2, TILE, TILE), v32(2, TILE, TILE), v32(2, TILE, TILE),
            v32(2, 2, MARGIN, CORE), v32(2, CORE, HALF), v32(2, TILE, HALF),
            v32(2, 3, 2, WIDE, HALF), v32(2, 3, 2, WIDE, HALF),
            v32(2, 576, HALF), v32(2, 576, HALF),
            v32(2, 3, 2, MARGIN, HALF), v32(2, 3, 2, MARGIN, HALF),
            v32(2, CORE, HALF), v32(2, CORE, HALF),
            pltpu.SemaphoreType.DMA((6,)),
            pltpu.SemaphoreType.DMA((28,)),
            pltpu.SemaphoreType.DMA((28,)),
        ],
        compiler_params=pltpu.CompilerParams(
            collective_id=0, has_side_effects=True, vmem_limit_bytes=60 * 1024 * 1024),
        name="ptycho",
    )(jnp.swapaxes(offsets, 2, 3), counts, object_field, probe, amplitudes, table, table_t, swap)


def solution(mesh):
    return jax.shard_map(
        shards,
        mesh=mesh,
        in_specs=(
            P(None, "row", "col"),
            P(),
            P("row", "col", None, None, None),
            P("row", "col", None, None),
            P("row", "col"),
        ),
        out_specs=P(None, "row", "col"),
        check_vma=False,
    )
```

time: 86.5 us -> 78.8 us (0.911)
  Pallas kernels: 82.8 us -> 75.8 us
    pallas_call x1, Pallas kernels: 82.8 us -> 75.8 us  [shards(): pl.pallas_call(kernel, out_shape=jax.ShapeDtypeStruct(object_field.shape,...]
    unnamed x4 -> x1, local copies, waits for them, and re-layouts: 2.82 us -> 2.14 us
where the time goes in v2:
time: 78.8 us; the launch traced here: 78.6 us
  Pallas kernels  75.8 us (96%)
  local copies, waits for them, and re-layouts  2.14 us (3%)
    pallas_call x1, Pallas kernels, shards(): pl.pallas_call(kernel, out_shape=jax.ShapeDtypeStruct(object_field.shape,...  75.8 us
    unnamed x1, local copies, waits for them, and re-layouts  2.14 us

profile of v2, /device:TPU:45, one launch (start us, length us, event | category | flops | bytes accessed | tf_op | source)
XLA Modules:
  0.0 78.6 jit_solution(8627343266645570072)
XLA Ops:
  0.7 75.8 %ptycho.1 = f32[2,288,288]{2,1,0:T(8,128)} custom-call(s32[1,1,2,8]{3,2,1,0:T(2,128)} %bitcast.1, s32[1,1]{1,0:T(1,128)S(6)} %copy.10.cnt, f32[2,288,288]{2,1,0:T(8,128)} %obj.1, f32[2,256,256]{2,1,0:T(8,128)} %probe.1, bf16[1,1,8,256,256]{4,3,2,1,0:T(8,128)(2,1)} %amp.1, bf16[256,256]{1,0:T(8,128)(2,1)} %constant.6.clone.table, ...), custom_call_target="tpu_custom_call" | custom-call | tf_op jit(solution)/shard_map/ptycho/pallas_call | solution.py:554
  76.5 2.1 %copy.11 = f32[2,288,288]{2,1,0:T(8,128)} copy(f32[2,288,288]{2,1,0:T(8,128)} %ptycho.1) | data formatting | bytes 1327104

commit v3 on v2

--- a/solution.py
+++ b/solution.py
@@ -35,7 +35,8 @@
     order = np.concatenate([np.arange(HALF), [HALF], np.arange(SIDE - 1, HALF, -1)])
     swap = np.zeros((SIDE, SIDE), np.float32)
     swap[np.arange(SIDE), order] = 1.0
-    return [a.astype(jnp.bfloat16) for a in (table, table.T, swap)]
+    paired = np.stack([table[:HALF].reshape(8, 16, SIDE), table[HALF:].reshape(8, 16, SIDE)], 1).reshape(SIDE, SIDE)
+    return [a.astype(jnp.bfloat16) for a in (table, table.T, paired, swap)]
 
 
 def mm(a, b):
@@ -55,10 +56,10 @@
 
 
 def kernel(
-    off, cnt, obj, probe, amp, table, table_t, swap, out,
-    ob, pb, ab, tv, ttv, sv,
+    off, cnt, obj, probe, amp, table, table_t, paired, swap, out,
+    ob, pb, ab, tv, ttv, tpv, sv,
     pr, ap, hb, wb, qb, xb, cur, ga, gb,
-    row_in, col_s, col_in, grow_s, grow_in, gcol_s, gcol_in, frow_s, frow_in, fcol_s, fcol_in,
+    row_in, tail_s, tail_in, col_s, col_in, grow_s, grow_in, gcol_s, gcol_in, frow_s, frow_in, fcol_s, fcol_in,
     load_sem, send_sem, recv_sem,
 ):
     n_row, n_col = lax.axis_size("row"), lax.axis_size("col")
@@ -80,7 +81,7 @@
     loads = [
         pltpu.make_async_copy(src, dst, load_sem.at[i])
         for i, (src, dst) in enumerate(
-            ((obj, ob), (probe, pb), (amp, ab), (table, tv), (table_t, ttv), (swap, sv))
+            ((obj, ob), (probe, pb), (amp, ab), (table, tv), (table_t, ttv), (paired, tpv), (swap, sv))
         )
     ]
     for copy in loads:
@@ -93,8 +94,6 @@
         @pl.when(ok)
         def _(device=device):
             pl.semaphore_signal(barrier, inc=1, device_id=device, device_id_type=pl.DeviceIdType.MESH)
-    pl.semaphore_wait(barrier, sum(peer(key)[0].astype(jnp.int32) for key in sides + corners))
-
     kinds, started = {}, []
 
     def semaphore(kind, key):
@@ -123,46 +122,56 @@
             remote(key, kind, src, dst, False).wait_recv()
 
     loads[0].wait()
-    for side in (0, 1):
-        start = 0 if side == 0 else CORE - MARGIN
-        send(("row", side), 0, ob.at[:, pl.ds(start, MARGIN), :], row_in.at[1 - side])
+
+    def own_rows(ref, comp, rows, n):
+        tail = jnp.concatenate([ref[comp, rows, pl.ds(256, 32)], jnp.zeros((n, 96), F32)], 1)
+        return ref[comp, rows, blk(0)], ref[comp, rows, blk(1)], tail
 
     def halo_col_pack(row, n):
         lane, rows = lane_iota(n), pl.ds(row, n)
-        re, im = ([ob[comp, rows, blk(0)], ob[comp, rows, blk(1)], ob[comp, rows, pl.ds(256, 32)]] for comp in (0, 1))
-        zero = jnp.zeros((n, 96), F32)
+        re, im = (own_rows(ob, comp, rows, n) for comp in (0, 1))
         col_s[0, rows, :] = jnp.where(lane < 64, re[0], pltpu.roll(im[0], 64, 1))
-        tail = [jnp.where(lane < 32, jnp.concatenate([v[2], zero], 1), v[1]) for v in (re, im)]
+        tail = [jnp.where(lane < 32, v[2], v[1]) for v in (re, im)]
         col_s[1, rows, :] = jnp.where(lane < 64, pltpu.roll(tail[0], 16, 1), pltpu.roll(tail[1], 80, 1))
 
-    for row in (0, CORE - MARGIN):
-        halo_col_pack(row, MARGIN)
-    for a, b in corners:
-        send((a, b), 1, col_s.at[b, pl.ds(0 if a == 0 else CORE - MARGIN, MARGIN), :],
-             col_in.at[1 - b, pl.ds(CORE + (1 - a) * MARGIN, MARGIN), :])
-
-    @pl.loop(1, CORE // MARGIN - 1)
+    def row_start(side):
+        return 0 if side == 0 else CORE - MARGIN
+
+    for side in (0, 1):
+        part = [
+            pltpu.roll(own_rows(ob, comp, pl.ds(row_start(side) + 24 * h, 24), 24)[2], 32 * (2 * h + comp), 1)
+            if h + comp else own_rows(ob, comp, pl.ds(row_start(side), 24), 24)[2]
+            for h in (0, 1) for comp in (0, 1)
+        ]
+        tail_s[side] = part[0] + part[1] + part[2] + part[3]
+
+    @pl.loop(0, CORE // MARGIN)
     def _(i):
         halo_col_pack(pl.multiple_of(i * MARGIN, MARGIN), MARGIN)
 
+    pl.semaphore_wait(barrier, sum(peer(key)[0].astype(jnp.int32) for key in sides + corners))
+
+    for side in (0, 1):
+        send(("row", side), 0, ob.at[:, pl.ds(row_start(side), MARGIN), pl.ds(0, SIDE)], row_in.at[1 - side])
+        send(("row", side), 7, tail_s.at[side], tail_in.at[1 - side])
+    for a, b in corners:
+        send((a, b), 1, col_s.at[b, pl.ds(row_start(a), MARGIN), :],
+             col_in.at[1 - b, pl.ds(CORE + (1 - a) * MARGIN, MARGIN), :])
     for side in (0, 1):
         send(("col", side), 2, col_s.at[side, :, :], col_in.at[1 - side, pl.ds(0, CORE), :])
 
-    def place_rows(ref, n, first):
-        @pl.loop(0, n // MARGIN)
-        def _(i):
-            at = pl.multiple_of(i * MARGIN, MARGIN)
-            rows, to_rows = pl.ds(at, MARGIN), pl.ds(first + at, MARGIN)
-            lane = lane_iota(MARGIN)
-            for comp in (0, 1):
-                a, b = (pltpu.roll(ref[comp, rows, blk(k)], MARGIN, 1) for k in (0, 1))
-                c = pltpu.roll(
-                    jnp.concatenate([ref[comp, rows, pl.ds(256, 32)], jnp.zeros((MARGIN, 96), F32)], 1), MARGIN, 1)
-                cur[comp, to_rows, blk(0)] = jnp.where(lane < MARGIN, 0.0, a)
-                cur[comp, to_rows, blk(1)] = jnp.where(lane < MARGIN, a, b)
-                cur[comp, to_rows, blk(2)] = jnp.where(lane < MARGIN, b, c)
-
-    place_rows(ob, CORE, MARGIN)
+    def place(comp, rows, values):
+        lane = lane_iota(values[0].shape[0])
+        a, b, c = (pltpu.roll(v, MARGIN, 1) for v in values)
+        cur[comp, rows, blk(0)] = jnp.where(lane < MARGIN, 0.0, a)
+        cur[comp, rows, blk(1)] = jnp.where(lane < MARGIN, a, b)
+        cur[comp, rows, blk(2)] = jnp.where(lane < MARGIN, b, c)
+
+    @pl.loop(0, CORE // MARGIN)
+    def _(i):
+        at = pl.multiple_of(i * MARGIN, MARGIN)
+        for comp in (0, 1):
+            place(comp, pl.ds(MARGIN + at, MARGIN), own_rows(ob, comp, pl.ds(at, MARGIN), MARGIN))
 
     def halo_col_unpack(side, row, at, n):
         lane, rows = lane_iota(n), pl.ds(row, n)
@@ -217,24 +226,22 @@
                 patch.append((jnp.where(hi_c, three[2], three[0]), three[1]))
             for b in (0, 1):
                 p0, p1 = pr[s, 0, pl.ds(m, 16), blk(b)], pr[s, 1, pl.ds(m, 16), blk(b)]
-                xb[buf, pl.ds(at, 16), blk(b)] = (p0 * patch[0][b] - p1 * patch[1][b]).astype(BF16)
-                xb[buf, pl.ds(HALF + at, 16), blk(b)] = (p0 * patch[1][b] + p1 * patch[0][b]).astype(BF16)
+                xb[buf, pl.ds(2 * at, 16), blk(b)] = (p0 * patch[0][b] - p1 * patch[1][b]).astype(BF16)
+                xb[buf, pl.ds(2 * at + 16, 16), blk(b)] = (p0 * patch[1][b] + p1 * patch[0][b]).astype(BF16)
         v = mm(xb[buf], ttv[...])
         for at in range(0, HALF, 16):
             rows = pl.ds(first + at, 16)
-            c_r, s_r = v[at : at + 16, :HALF], v[at : at + 16, HALF:]
-            c_i, s_i = v[HALF + at : HALF + at + 16, :HALF], v[HALF + at : HALF + at + 16, HALF:]
+            re, im = slice(2 * at, 2 * at + 16), slice(2 * at + 16, 2 * at + 32)
+            c_r, s_r, c_i, s_i = v[re, :HALF], v[re, HALF:], v[im, :HALF], v[im, HALF:]
             hb[s, rows, blk(0)] = cols_fix(c_r + s_i, c_r, lane).astype(BF16)
             hb[s, rows, blk(1)] = cols_fix(c_r - s_i, s_r, lane).astype(BF16)
             hb[s, rows, blk(2)] = cols_fix(c_i - s_r, c_i, lane).astype(BF16)
             hb[s, rows, blk(3)] = cols_fix(c_i + s_r, s_i, lane).astype(BF16)
 
-    def middle(s, buf):
-        u = mm(tv[...], hb[s])
-        lane = lane_iota(16)
+    def correct(s, buf, u):
         for k in range(0, HALF, 16):
             for b in (0, 1):
-                lo, hi = slice(k, k + 16), slice(HALF + k, HALF + k + 16)
+                lo, hi = slice(2 * k, 2 * k + 16), slice(2 * k + 16, 2 * k + 32)
                 re, im = slice(b * HALF, b * HALF + HALF), slice(SIDE + b * HALF, SIDE + b * HALF + HALF)
                 c_r, s_r, c_i, s_i = u[lo, re], u[hi, re], u[lo, im], u[hi, im]
                 p_r, p_i, m_r, m_i = c_r + s_i, c_i - s_r, c_r - s_i, c_i + s_r
@@ -253,12 +260,13 @@
                 wb[buf, pl.ds(k, 16), blk(2 + b)] = a_i.astype(BF16)
                 wb[buf, pl.ds(HALF + k, 16), blk(b)] = nb_i.astype(BF16)
                 wb[buf, pl.ds(HALF + k, 16), blk(2 + b)] = b_r.astype(BF16)
-        y = mm(ttv[...], wb[buf])
+
+    def split_columns(s, y):
+        lane = lane_iota(16)
         for m in range(0, SIDE, 16):
             rows = slice(m, m + 16)
             p_r, m_r, p_i, m_i = (y[rows, b * HALF : b * HALF + HALF] for b in range(4))
-            re = m if m < HALF else HALF + m
-            im = re + HALF
+            re, im = 2 * m, 2 * m + 16
             qb[s, pl.ds(re, 16), blk(0)] = cols_fix(p_r + m_r, p_r, lane).astype(BF16)
             qb[s, pl.ds(re, 16), blk(1)] = cols_fix(m_i - p_i, m_r, lane).astype(BF16)
             qb[s, pl.ds(im, 16), blk(0)] = cols_fix(p_i + m_i, p_i, lane).astype(BF16)
@@ -275,8 +283,8 @@
                 r, c = off[0, 0, 0, slot], off[0, 0, 1, slot]
                 terms = ([], [])
                 for b in (0, 1):
-                    b_r = v[at : at + 16, b * HALF : b * HALF + HALF]
-                    b_i = v[HALF + at : HALF + at + 16, b * HALF : b * HALF + HALF]
+                    b_r = v[2 * at : 2 * at + 16, b * HALF : b * HALF + HALF]
+                    b_i = v[2 * at + 16 : 2 * at + 32, b * HALF : b * HALF + HALF]
                     p0, p1 = pr[slot, 0, pl.ds(m, 16), blk(b)], pr[slot, 1, pl.ds(m, 16), blk(b)]
                     terms[0].append(p0 * b_r + p1 * b_i)
                     terms[1].append(p0 * b_i - p1 * b_r)
@@ -301,11 +309,20 @@
             for buf in (0, 1):
                 forward_rows(2 * i + buf, first, buf)
 
-    def middles():
+    def edge_pass(g):
         @pl.loop(0, SLOTS // 2)
         def _(i):
+            pair = (2 * i, 2 * i + 1)
             for buf in (0, 1):
-                middle(2 * i + buf, buf)
+                forward_rows(pair[buf], EDGE, buf)
+            far = [mm(tpv[...], hb[s]) for s in pair]
+            back = []
+            for buf in (0, 1):
+                correct(pair[buf], buf, far[buf])
+                back.append(mm(ttv[...], wb[buf]))
+            for buf in (0, 1):
+                split_columns(pair[buf], back[buf])
+            backward_rows(pair, EDGE, g)
 
     def backward(first, g):
         @pl.loop(0, SLOTS // 2)
@@ -326,11 +343,20 @@
 
     for side in (0, 1):
         first = 0 if side == 0 else TILE - MARGIN
-        arrived(("row", side), 0, ob.at[:, pl.ds(0, MARGIN), :], row_in.at[side])
+        arrived(("row", side), 0, ob.at[:, pl.ds(0, MARGIN), pl.ds(0, SIDE)], row_in.at[side])
+        arrived(("row", side), 7, tail_s.at[1 - side], tail_in.at[side])
 
         @pl.when(has["row", side])
         def _(side=side, first=first):
-            place_rows(row_in.at[side], MARGIN, first)
+            lane = lane_iota(24)
+            for h in (0, 1):
+                for comp in (0, 1):
+                    shift = (HALF - 32 * (2 * h + comp)) % HALF
+                    tail = tail_in[side] if shift == 0 else pltpu.roll(tail_in[side], shift, 1)
+                    rows = pl.ds(24 * h, 24)
+                    place(comp, pl.ds(first + 24 * h, 24),
+                          (row_in[side, comp, rows, blk(0)], row_in[side, comp, rows, blk(1)],
+                           jnp.where(lane < 32, tail, 0.0)))
 
         @pl.when(jnp.logical_not(has["row", side]))
         def _(first=first):
@@ -344,9 +370,7 @@
         def _(a=a, b=b, at=at):
             halo_col_unpack(b, a * (TILE - MARGIN), at, MARGIN)
 
-    forward(EDGE)
-    middles()
-    backward(EDGE, ga)
+    edge_pass(ga)
 
     def stage(dst, g, src_row, n_rows):
         for b in range(3):
@@ -468,9 +492,7 @@
     gcol_add(1)
     update((0, MARGIN, TILE - WIDE, TILE - MARGIN))
 
-    forward(EDGE)
-    middles()
-    backward(EDGE, gb)
+    edge_pass(gb)
     for side in (0, 1):
         stage(frow_s.at[side], gb, 0 if side == 0 else TILE - MARGIN, MARGIN)
     send_rows(frow_s, frow_in, ("f",))
@@ -546,7 +568,7 @@
 
 
 def shards(object_field, probe, amplitudes, offsets, counts):
-    table, table_t, swap = (jnp.asarray(a) for a in half_tables())
+    tables = (jnp.asarray(a) for a in half_tables())
     anywhere = pl.BlockSpec(memory_space=pl.ANY)
     scalars = pl.BlockSpec(memory_space=pltpu.SMEM)
     v32 = lambda *shape: pltpu.VMEM(shape, F32)
@@ -554,27 +576,27 @@
     return pl.pallas_call(
         kernel,
         out_shape=jax.ShapeDtypeStruct(object_field.shape, F32),
-        in_specs=[scalars, scalars] + [anywhere] * 6,
+        in_specs=[scalars, scalars] + [anywhere] * 7,
         out_specs=pl.BlockSpec(memory_space=pltpu.VMEM),
         scratch_shapes=[
             v32(2, CORE, CORE), v32(2, SIDE, SIDE), v16(1, 1, SLOTS, SIDE, SIDE),
-            v16(SIDE, SIDE), v16(SIDE, SIDE), v16(SIDE, SIDE),
+            v16(SIDE, SIDE), v16(SIDE, SIDE), v16(SIDE, SIDE), v16(SIDE, SIDE),
             v32(SLOTS, 2, SIDE, SIDE), v16(SLOTS, SIDE, SIDE),
             v16(SLOTS, SIDE, 2 * SIDE), v16(2, SIDE, 2 * SIDE), v16(SLOTS, 2 * SIDE, SIDE), v16(2, SIDE, SIDE),
             v32(2, TILE, TILE), v32(2, TILE, TILE), v32(2, TILE, TILE),
-            v32(2, 2, MARGIN, CORE), v32(2, CORE, HALF), v32(2, TILE, HALF),
+            v32(2, 2, MARGIN, SIDE), v32(2, MARGIN // 2, HALF), v32(2, MARGIN // 2, HALF), v32(2, CORE, HALF), v32(2, TILE, HALF),
             v32(2, 3, 2, WIDE, HALF), v32(2, 3, 2, WIDE, HALF),
             v32(2, 576, HALF), v32(2, 576, HALF),
             v32(2, 3, 2, MARGIN, HALF), v32(2, 3, 2, MARGIN, HALF),
             v32(2, CORE, HALF), v32(2, CORE, HALF),
-            pltpu.SemaphoreType.DMA((6,)),
-            pltpu.SemaphoreType.DMA((28,)),
-            pltpu.SemaphoreType.DMA((28,)),
+            pltpu.SemaphoreType.DMA((7,)),
+            pltpu.SemaphoreType.DMA((30,)),
+            pltpu.SemaphoreType.DMA((30,)),
         ],
         compiler_params=pltpu.CompilerParams(
             collective_id=0, has_side_effects=True, vmem_limit_bytes=60 * 1024 * 1024),
         name="ptycho",
-    )(jnp.swapaxes(offsets, 2, 3), counts, object_field, probe, amplitudes, table, table_t, swap)
+    )(jnp.swapaxes(offsets, 2, 3), counts, object_field, probe, amplitudes, *tables)
 
 
 def solution(mesh):

time: 78.8 us -> 73.5 us (0.933)
  Pallas kernels: 75.8 us -> 70.3 us
    pallas_call x1, Pallas kernels: 75.8 us -> 70.3 us  [shards(): pl.pallas_call(kernel, out_shape=jax.ShapeDtypeStruct(object_field.shape,...]
where the time goes in v3:
time: 73.5 us; the launch traced here: 73.1 us
  Pallas kernels  70.3 us (96%)
  local copies, waits for them, and re-layouts  2.14 us (3%)
    pallas_call x1, Pallas kernels, shards(): pl.pallas_call(kernel, out_shape=jax.ShapeDtypeStruct(object_field.shape,...  70.3 us
    unnamed x1, local copies, waits for them, and re-layouts  2.14 us

profile of v3, /device:TPU:45, one launch (start us, length us, event | category | flops | bytes accessed | tf_op | source)
XLA Modules:
  0.0 73.1 jit_solution(3934280798996425743)
XLA Ops:
  0.7 70.3 %ptycho.1 = f32[2,288,288]{2,1,0:T(8,128)} custom-call(s32[1,1,2,8]{3,2,1,0:T(2,128)} %bitcast.1, s32[1,1]{1,0:T(1,128)S(6)} %copy.11.cnt, f32[2,288,288]{2,1,0:T(8,128)} %obj.1, f32[2,256,256]{2,1,0:T(8,128)} %probe.1, bf16[1,1,8,256,256]{4,3,2,1,0:T(8,128)(2,1)} %amp.1, bf16[256,256]{1,0:T(8,128)(2,1)} %constant.8.clone.table, ...), custom_call_target="tpu_custom_call" | custom-call | tf_op jit(solution)/shard_map/ptycho/pallas_call | solution.py:576
  71.0 2.1 %copy.12 = f32[2,288,288]{2,1,0:T(8,128)} copy(f32[2,288,288]{2,1,0:T(8,128)} %ptycho.1) | data formatting | bytes 1327104

commit v4 on v3

--- a/solution.py
+++ b/solution.py
@@ -22,6 +22,7 @@
 BF16 = jnp.bfloat16
 
 WIDE = 2 * MARGIN
+QUARTER = CORE // 4
 
 EDGE, INNER = 0, HALF
 
@@ -59,7 +60,7 @@
     off, cnt, obj, probe, amp, table, table_t, paired, swap, out,
     ob, pb, ab, tv, ttv, tpv, sv,
     pr, ap, hb, wb, qb, xb, cur, ga, gb,
-    row_in, tail_s, tail_in, col_s, col_in, grow_s, grow_in, gcol_s, gcol_in, frow_s, frow_in, fcol_s, fcol_in,
+    row_in, tail_s, tail_in, col_s, col_in, corner_s, corner_in, grow_s, grow_in, gcol_s, gcol_in, frow_s, frow_in, fcol_s, fcol_in,
     load_sem, send_sem, recv_sem,
 ):
     n_row, n_col = lax.axis_size("row"), lax.axis_size("col")
@@ -127,12 +128,30 @@
         tail = jnp.concatenate([ref[comp, rows, pl.ds(256, 32)], jnp.zeros((n, 96), F32)], 1)
         return ref[comp, rows, blk(0)], ref[comp, rows, blk(1)], tail
 
-    def halo_col_pack(row, n):
-        lane, rows = lane_iota(n), pl.ds(row, n)
-        re, im = (own_rows(ob, comp, rows, n) for comp in (0, 1))
-        col_s[0, rows, :] = jnp.where(lane < 64, re[0], pltpu.roll(im[0], 64, 1))
-        tail = [jnp.where(lane < 32, v[2], v[1]) for v in (re, im)]
-        col_s[1, rows, :] = jnp.where(lane < 64, pltpu.roll(tail[0], 16, 1), pltpu.roll(tail[1], 80, 1))
+    def rolled(value, shift):
+        return pltpu.roll(value, shift % HALF, 1) if shift % HALF else value
+
+    def pack(dst, base, strips):
+        n = strips[0].shape[0]
+        lane = lane_iota(n)
+        for k in range(3):
+            dst[pl.ds(base + k * n, n), :] = jnp.where(lane < 96, strips[k], rolled(strips[3], 96 - 32 * k))
+
+    def unpack(src, base, n):
+        lane = lane_iota(n)
+        three = [src[pl.ds(base + k * n, n), :] for k in range(3)]
+        a, b, c = (rolled(v, 32 * k + 32) for k, v in enumerate(three))
+        return three + [jnp.where(lane < 32, a, jnp.where(lane < 64, b, c))]
+
+    def pair_up(re, im, at):
+        return jnp.where(lane_iota(re.shape[0]) < MARGIN, rolled(re, -at), rolled(im, MARGIN - at))
+
+    def own_strip(side, row, n):
+        re, im = (own_rows(ob, comp, pl.ds(row, n), n) for comp in (0, 1))
+        if side == 0:
+            return pair_up(re[0], im[0], 0)
+        lane = lane_iota(n)
+        return pair_up(*(jnp.where(lane < 32, v[2], v[1]) for v in (re, im)), 112)
 
     def row_start(side):
         return 0 if side == 0 else CORE - MARGIN
@@ -145,9 +164,10 @@
         ]
         tail_s[side] = part[0] + part[1] + part[2] + part[3]
 
-    @pl.loop(0, CORE // MARGIN)
-    def _(i):
-        halo_col_pack(pl.multiple_of(i * MARGIN, MARGIN), MARGIN)
+    for b in (0, 1):
+        for a in (0, 1):
+            corner_s[b, a] = own_strip(b, row_start(a), MARGIN)
+        pack(col_s.at[b], 0, [own_strip(b, k * QUARTER, QUARTER) for k in range(4)])
 
     pl.semaphore_wait(barrier, sum(peer(key)[0].astype(jnp.int32) for key in sides + corners))
 
@@ -155,10 +175,9 @@
         send(("row", side), 0, ob.at[:, pl.ds(row_start(side), MARGIN), pl.ds(0, SIDE)], row_in.at[1 - side])
         send(("row", side), 7, tail_s.at[side], tail_in.at[1 - side])
     for a, b in corners:
-        send((a, b), 1, col_s.at[b, pl.ds(row_start(a), MARGIN), :],
-             col_in.at[1 - b, pl.ds(CORE + (1 - a) * MARGIN, MARGIN), :])
+        send((a, b), 1, corner_s.at[b, a], corner_in.at[1 - b, 1 - a])
     for side in (0, 1):
-        send(("col", side), 2, col_s.at[side, :, :], col_in.at[1 - side, pl.ds(0, CORE), :])
+        send(("col", side), 2, col_s.at[side], col_in.at[1 - side])
 
     def place(comp, rows, values):
         lane = lane_iota(values[0].shape[0])
@@ -173,16 +192,16 @@
         for comp in (0, 1):
             place(comp, pl.ds(MARGIN + at, MARGIN), own_rows(ob, comp, pl.ds(at, MARGIN), MARGIN))
 
-    def halo_col_unpack(side, row, at, n):
+    def place_columns(side, row, strip):
+        n = strip.shape[0]
         lane, rows = lane_iota(n), pl.ds(row, n)
-        strip = col_in[side, pl.ds(at, n), :]
-        if side == 0:
-            for comp, shift in ((0, 0), (1, 64)):
-                new = strip if shift == 0 else pltpu.roll(strip, shift, 1)
-                cur[comp, rows, blk(0)] = jnp.where(lane < 48, new, cur[comp, rows, blk(0)])
-        else:
-            for comp, shift in ((0, 80), (1, 16)):
-                cur[comp, rows, blk(2)] = jnp.where(lane >= 80, pltpu.roll(strip, shift, 1), cur[comp, rows, blk(2)])
+        for comp in (0, 1):
+            if side == 0:
+                new = rolled(strip, -MARGIN * comp)
+                cur[comp, rows, blk(0)] = jnp.where(lane < MARGIN, new, cur[comp, rows, blk(0)])
+            else:
+                new = rolled(strip, 80 - MARGIN * comp)
+                cur[comp, rows, blk(2)] = jnp.where(lane >= 80, new, cur[comp, rows, blk(2)])
 
     @pl.loop(0, TILE // MARGIN)
     def _(i):
@@ -202,7 +221,7 @@
         live = jnp.where(s < live_count, 1.0, 0.0).astype(F32)
         for comp in (0, 1):
             pr[s, comp] = pltpu.roll(pltpu.roll(pb[comp], r, 0), c, 1) * live
-        ap[s] = mm(mm(sv[...], ab[0, 0, s]).astype(BF16), sv[...]).astype(BF16)
+        ap[s] = mm(mm(sv[...], ab[0, 0, s]).astype(BF16), sv[...])
 
     def cols_fix(plain, other, lane):
         return jnp.where(lane == 0, other, plain)
@@ -249,8 +268,8 @@
                     first = row_iota(16, 0) == 0
                     p_r, p_i = jnp.where(first, c_r, p_r), jnp.where(first, c_i, p_i)
                     m_r, m_i = jnp.where(first, s_r, m_r), jnp.where(first, s_i, m_i)
-                f_p = ap[s, pl.ds(k, 16), blk(b)].astype(F32) * lax.rsqrt(p_r * p_r + p_i * p_i + FLOOR) - 1.0
-                f_m = ap[s, pl.ds(HALF + k, 16), blk(b)].astype(F32) * lax.rsqrt(m_r * m_r + m_i * m_i + FLOOR) - 1.0
+                f_p = ap[s, pl.ds(k, 16), blk(b)] * lax.rsqrt(p_r * p_r + p_i * p_i + FLOOR) - 1.0
+                f_m = ap[s, pl.ds(HALF + k, 16), blk(b)] * lax.rsqrt(m_r * m_r + m_i * m_i + FLOOR) - 1.0
                 p_r, p_i, m_r, m_i = p_r * f_p, p_i * f_p, m_r * f_m, m_i * f_m
                 a_r, a_i, nb_i, b_r = p_r + m_r, p_i + m_i, m_i - p_i, p_r - m_r
                 if k == 0:
@@ -330,14 +349,12 @@
             backward_rows((2 * i, 2 * i + 1), first, g)
 
     for side in (0, 1):
-        arrived(("col", side), 2, col_s.at[1 - side, :, :], col_in.at[side, pl.ds(0, CORE), :])
+        arrived(("col", side), 2, col_s.at[1 - side], col_in.at[side])
 
         @pl.when(has["col", side])
         def _(side=side):
-            @pl.loop(0, CORE // MARGIN)
-            def _(i):
-                at = pl.multiple_of(i * MARGIN, MARGIN)
-                halo_col_unpack(side, MARGIN + at, at, MARGIN)
+            for k, strip in enumerate(unpack(col_in.at[side], 0, QUARTER)):
+                place_columns(side, MARGIN + k * QUARTER, strip)
 
     forward(INNER)
 
@@ -363,12 +380,11 @@
             for comp in (0, 1):
                 cur[comp, pl.ds(first, MARGIN), :] = jnp.zeros((MARGIN, TILE), F32)
     for a, b in corners:
-        at = CORE + a * MARGIN
-        arrived((a, b), 1, col_s.at[1 - b, pl.ds(0, MARGIN), :], col_in.at[b, pl.ds(at, MARGIN), :])
+        arrived((a, b), 1, corner_s.at[1 - b, 1 - a], corner_in.at[b, a])
 
         @pl.when(peer((a, b))[0])
-        def _(a=a, b=b, at=at):
-            halo_col_unpack(b, a * (TILE - MARGIN), at, MARGIN)
+        def _(a=a, b=b):
+            place_columns(b, a * (TILE - MARGIN), corner_in[b, a])
 
     edge_pass(ga)
 
@@ -498,46 +514,38 @@
     send_rows(frow_s, frow_in, ("f",))
     backward(INNER, gb)
 
-    def fcol_index(part):
+    def fcol_rows(part):
         if part == 0:
-            return [(WIDE + j, j) for j in range(0, 192, MARGIN)]
-        return [(MARGIN, 192), (TILE - WIDE, 240)]
+            return 0, 48, [WIDE + 48 * k for k in range(4)]
+        return 144, 24, [MARGIN, MARGIN + 24, TILE - WIDE, TILE - WIDE + 24]
 
     def fcol_pack(part):
-        lane = lane_iota(MARGIN)
-        for row, at in fcol_index(part):
-            rows, to_rows = pl.ds(row, MARGIN), pl.ds(at, MARGIN)
-            fcol_s[0, to_rows, :] = jnp.where(
-                lane < 64, gb[0, rows, blk(0)], pltpu.roll(gb[1, rows, blk(0)], 64, 1))
-            fcol_s[1, to_rows, :] = jnp.where(
-                lane < 64, pltpu.roll(gb[0, rows, blk(2)], 48, 1), pltpu.roll(gb[1, rows, blk(2)], 112, 1))
-
-    def fcol_unpack(side, part):
-        lane = lane_iota(MARGIN)
-        for row, at in fcol_index(part):
-            strip = fcol_in[side, pl.ds(at, MARGIN), :]
-            if side == 0:
-                b, ok = 0, jnp.logical_and(lane >= 48, lane < 96)
-                pair = (pltpu.roll(strip, 48, 1), pltpu.roll(strip, 112, 1))
-            else:
-                b, ok = 2, jnp.logical_and(lane >= 32, lane < 80)
-                pair = (pltpu.roll(strip, 32, 1), pltpu.roll(strip, 96, 1))
-            for comp in (0, 1):
-                gb[comp, pl.ds(row, MARGIN), blk(b)] += jnp.where(ok, pair[comp], 0.0)
+        base, n, starts = fcol_rows(part)
+        for side in (0, 1):
+            pack(fcol_s.at[side], base, [
+                pair_up(*(gb[comp, pl.ds(row, n), blk(2 * side)] for comp in (0, 1)), 80 * side) for row in starts])
 
     def fcol_send(part):
-        rows = pl.ds(*((0, 192), (192, 96))[part])
-        for side in (0, 1):
+        base, n, _ = fcol_rows(part)
+        for side in (0, 1):
+            rows = pl.ds(base, 3 * n)
             send(("col", side), 5 + part, fcol_s.at[side, rows, :], fcol_in.at[1 - side, rows, :])
 
     def fcol_add(part):
-        rows = pl.ds(*((0, 192), (192, 96))[part])
+        base, n, starts = fcol_rows(part)
+        rows = pl.ds(base, 3 * n)
         for side in (0, 1):
             arrived(("col", side), 5 + part, fcol_s.at[1 - side, rows, :], fcol_in.at[side, rows, :])
 
             @pl.when(has["col", side])
             def _(side=side):
-                fcol_unpack(side, part)
+                first = MARGIN if side == 0 else 32
+                lane = lane_iota(n)
+                ok = jnp.logical_and(lane >= first, lane < first + MARGIN)
+                for row, strip in zip(starts, unpack(fcol_in.at[side], base, n)):
+                    for comp in (0, 1):
+                        gb[comp, pl.ds(row, n), blk(2 * side)] += jnp.where(
+                            ok, rolled(strip, first - MARGIN * comp), 0.0)
 
     def write(row):
         lane, rows, to_rows = lane_iota(MARGIN), pl.ds(row, MARGIN), pl.ds(row - MARGIN, MARGIN)
@@ -581,14 +589,15 @@
         scratch_shapes=[
             v32(2, CORE, CORE), v32(2, SIDE, SIDE), v16(1, 1, SLOTS, SIDE, SIDE),
             v16(SIDE, SIDE), v16(SIDE, SIDE), v16(SIDE, SIDE), v16(SIDE, SIDE),
-            v32(SLOTS, 2, SIDE, SIDE), v16(SLOTS, SIDE, SIDE),
+            v32(SLOTS, 2, SIDE, SIDE), v32(SLOTS, SIDE, SIDE),
             v16(SLOTS, SIDE, 2 * SIDE), v16(2, SIDE, 2 * SIDE), v16(SLOTS, 2 * SIDE, SIDE), v16(2, SIDE, SIDE),
             v32(2, TILE, TILE), v32(2, TILE, TILE), v32(2, TILE, TILE),
-            v32(2, 2, MARGIN, SIDE), v32(2, MARGIN // 2, HALF), v32(2, MARGIN // 2, HALF), v32(2, CORE, HALF), v32(2, TILE, HALF),
+            v32(2, 2, MARGIN, SIDE), v32(2, MARGIN // 2, HALF), v32(2, MARGIN // 2, HALF), v32(2, 3 * QUARTER, HALF), v32(2, 3 * QUARTER, HALF),
+            v32(2, 2, MARGIN, HALF), v32(2, 2, MARGIN, HALF),
             v32(2, 3, 2, WIDE, HALF), v32(2, 3, 2, WIDE, HALF),
             v32(2, 576, HALF), v32(2, 576, HALF),
             v32(2, 3, 2, MARGIN, HALF), v32(2, 3, 2, MARGIN, HALF),
-            v32(2, CORE, HALF), v32(2, CORE, HALF),
+            v32(2, 216, HALF), v32(2, 216, HALF),
             pltpu.SemaphoreType.DMA((7,)),
             pltpu.SemaphoreType.DMA((30,)),
             pltpu.SemaphoreType.DMA((30,)),

time: 73.5 us -> 71.9 us (0.978); the launches traced: 73.1 us -> 70.5 us
  Pallas kernels: 70.3 us -> 67.7 us
    pallas_call x1, Pallas kernels: 70.3 us -> 67.7 us  [shards(): pl.pallas_call(kernel, out_shape=jax.ShapeDtypeStruct(object_field.shape,...]
where the time goes in v4:
time: 71.9 us; the launch traced here: 70.5 us
  Pallas kernels  67.7 us (94%)
  local copies, waits for them, and re-layouts  2.14 us (3%)
    pallas_call x1, Pallas kernels, shards(): pl.pallas_call(kernel, out_shape=jax.ShapeDtypeStruct(object_field.shape,...  67.7 us
    unnamed x1, local copies, waits for them, and re-layouts  2.14 us

profile of v4, /device:TPU:45, one launch (start us, length us, event | category | flops | bytes accessed | tf_op | source)
XLA Modules:
  0.0 70.5 jit_solution(1526503310138055104)
XLA Ops:
  0.7 67.7 %ptycho.1 = f32[2,288,288]{2,1,0:T(8,128)} custom-call(s32[1,1,2,8]{3,2,1,0:T(2,128)} %bitcast.1, s32[1,1]{1,0:T(1,128)S(6)} %copy.11.cnt, f32[2,288,288]{2,1,0:T(8,128)} %obj.1, f32[2,256,256]{2,1,0:T(8,128)} %probe.1, bf16[1,1,8,256,256]{4,3,2,1,0:T(8,128)(2,1)} %amp.1, bf16[256,256]{1,0:T(8,128)(2,1)} %constant.8.clone.table, ...), custom_call_target="tpu_custom_call" | custom-call | tf_op jit(solution)/shard_map/ptycho/pallas_call | solution.py:584
  68.4 2.1 %copy.12 = f32[2,288,288]{2,1,0:T(8,128)} copy(f32[2,288,288]{2,1,0:T(8,128)} %ptycho.1) | data formatting | bytes 1327104

commit v5 on v4

--- a/solution.py
+++ b/solution.py
@@ -172,12 +172,12 @@
     pl.semaphore_wait(barrier, sum(peer(key)[0].astype(jnp.int32) for key in sides + corners))
 
     for side in (0, 1):
+        send(("col", side), 2, col_s.at[side], col_in.at[1 - side])
+    for side in (0, 1):
         send(("row", side), 0, ob.at[:, pl.ds(row_start(side), MARGIN), pl.ds(0, SIDE)], row_in.at[1 - side])
         send(("row", side), 7, tail_s.at[side], tail_in.at[1 - side])
     for a, b in corners:
         send((a, b), 1, corner_s.at[b, a], corner_in.at[1 - b, 1 - a])
-    for side in (0, 1):
-        send(("col", side), 2, col_s.at[side], col_in.at[1 - side])
 
     def place(comp, rows, values):
         lane = lane_iota(values[0].shape[0])
@@ -393,12 +393,10 @@
             for comp in (0, 1):
                 dst[b, comp] = g[comp, pl.ds(src_row, n_rows), blk(b)]
 
-    def send_rows(src, dst, kind):
+    def send_rows(src, dst, kind, blocks):
         for side in (0, 1):
-            for b in (0, 2):
+            for b in blocks:
                 send(("row", side), kind + (b,), src.at[side, b], dst.at[1 - side, b])
-        for side in (0, 1):
-            send(("row", side), kind + (1,), src.at[side, 1], dst.at[1 - side, 1])
 
     def add_rows(src, dst, kind, g, first, n_rows, blocks):
         for side in (0, 1):
@@ -413,7 +411,7 @@
 
     for side in (0, 1):
         stage(grow_s.at[side], ga, 0 if side == 0 else TILE - WIDE, WIDE)
-    send_rows(grow_s, grow_in, ("g",))
+    send_rows(grow_s, grow_in, ("g",), (0, 2))
     backward(INNER, ga)
 
     def gcol_index(part):
@@ -496,22 +494,22 @@
 
     gcol_pack(0)
     gcol_send(0)
-    gcol_add(0)
-    update(range(WIDE, TILE - WIDE, MARGIN))
-    forward(INNER)
-
     first = (0, TILE - WIDE)
     add_rows(grow_s, grow_in, ("g",), ga, first, WIDE, (0, 2))
     gcol_pack(1)
     gcol_send(1)
+    send_rows(grow_s, grow_in, ("g",), (1,))
+    gcol_add(0)
+    update(range(WIDE, TILE - WIDE, MARGIN))
+    forward(INNER)
+    gcol_add(1)
     add_rows(grow_s, grow_in, ("g",), ga, first, WIDE, (1,))
-    gcol_add(1)
     update((0, MARGIN, TILE - WIDE, TILE - MARGIN))
 
     edge_pass(gb)
     for side in (0, 1):
         stage(frow_s.at[side], gb, 0 if side == 0 else TILE - MARGIN, MARGIN)
-    send_rows(frow_s, frow_in, ("f",))
+    send_rows(frow_s, frow_in, ("f",), (0, 2))
     backward(INNER, gb)
 
     def fcol_rows(part):
@@ -557,13 +555,14 @@
 
     fcol_pack(0)
     fcol_send(0)
-    fcol_add(0)
-    for row in range(WIDE, TILE - WIDE, MARGIN):
-        write(row)
+    send_rows(frow_s, frow_in, ("f",), (1,))
     first = (MARGIN, TILE - WIDE)
     add_rows(frow_s, frow_in, ("f",), gb, first, MARGIN, (0, 2))
     fcol_pack(1)
     fcol_send(1)
+    fcol_add(0)
+    for row in range(WIDE, TILE - WIDE, MARGIN):
+        write(row)
     add_rows(frow_s, frow_in, ("f",), gb, first, MARGIN, (1,))
     fcol_add(1)
     for row in first:

time: 71.9 us -> 67.6 us (0.940); the launches traced: 70.5 us -> 67.1 us
  Pallas kernels: 67.7 us -> 64.3 us
    pallas_call x1, Pallas kernels: 67.7 us -> 64.3 us  [shards(): pl.pallas_call(kernel, out_shape=jax.ShapeDtypeStruct(object_field.shape,...]
where the time goes in v5:
time: 67.6 us; the launch traced here: 67.1 us
  Pallas kernels  64.3 us (95%)
  local copies, waits for them, and re-layouts  2.14 us (3%)
    pallas_call x1, Pallas kernels, shards(): pl.pallas_call(kernel, out_shape=jax.ShapeDtypeStruct(object_field.shape,...  64.3 us
    unnamed x1, local copies, waits for them, and re-layouts  2.14 us

profile of v5, /device:TPU:45, one launch (start us, length us, event | category | flops | bytes accessed | tf_op | source)
XLA Modules:
  0.0 67.1 jit_solution(2381552874380053382)
XLA Ops:
  0.7 64.3 %ptycho.1 = f32[2,288,288]{2,1,0:T(8,128)} custom-call(s32[1,1,2,8]{3,2,1,0:T(2,128)} %bitcast.1, s32[1,1]{1,0:T(1,128)S(6)} %copy.11.cnt, f32[2,288,288]{2,1,0:T(8,128)} %obj.1, f32[2,256,256]{2,1,0:T(8,128)} %probe.1, bf16[1,1,8,256,256]{4,3,2,1,0:T(8,128)(2,1)} %amp.1, bf16[256,256]{1,0:T(8,128)(2,1)} %constant.8.clone.table, ...), custom_call_target="tpu_custom_call" | custom-call | tf_op jit(solution)/shard_map/ptycho/pallas_call | solution.py:583
  65.0 2.1 %copy.12 = f32[2,288,288]{2,1,0:T(8,128)} copy(f32[2,288,288]{2,1,0:T(8,128)} %ptycho.1) | data formatting | bytes 1327104

commit v6 on v5

--- a/solution.py
+++ b/solution.py
@@ -329,19 +329,37 @@
                 forward_rows(2 * i + buf, first, buf)
 
     def edge_pass(g):
-        @pl.loop(0, SLOTS // 2)
-        def _(i):
-            pair = (2 * i, 2 * i + 1)
+        def pair(i):
+            return 2 * i, 2 * i + 1
+
+        def first(i):
             for buf in (0, 1):
-                forward_rows(pair[buf], EDGE, buf)
-            far = [mm(tpv[...], hb[s]) for s in pair]
+                forward_rows(pair(i)[buf], EDGE, buf)
+
+        def middle(i, before, after):
+            far = [mm(tpv[...], hb[s]) for s in pair(i)]
+            before()
             back = []
             for buf in (0, 1):
-                correct(pair[buf], buf, far[buf])
+                correct(pair(i)[buf], buf, far[buf])
                 back.append(mm(ttv[...], wb[buf]))
+            after()
             for buf in (0, 1):
-                split_columns(pair[buf], back[buf])
-            backward_rows(pair, EDGE, g)
+                split_columns(pair(i)[buf], back[buf])
+
+        def last(i):
+            backward_rows(pair(i), EDGE, g)
+
+        nothing = lambda: None
+        end = SLOTS // 2 - 1
+        first(0)
+        middle(0, nothing, lambda: first(1))
+
+        @pl.loop(1, end)
+        def _(i):
+            middle(i, lambda: last(i - 1), lambda: first(i + 1))
+        middle(end, lambda: last(end - 1), nothing)
+        last(end)
 
     def backward(first, g):
         @pl.loop(0, SLOTS // 2)

time: 67.6 us -> 67 us (level)
  no operation moved by 1% of the time
where the time goes in v6:
time: 67 us; the launch traced here: 66.5 us
  Pallas kernels  63.7 us (95%)
  local copies, waits for them, and re-layouts  2.14 us (3%)
    pallas_call x1, Pallas kernels, shards(): pl.pallas_call(kernel, out_shape=jax.ShapeDtypeStruct(object_field.shape,...  63.7 us
    unnamed x1, local copies, waits for them, and re-layouts  2.14 us

profile of v6, /device:TPU:45, one launch (start us, length us, event | category | flops | bytes accessed | tf_op | source)
XLA Modules:
  0.0 66.5 jit_solution(18100884281831099589)
XLA Ops:
  0.7 63.7 %ptycho.1 = f32[2,288,288]{2,1,0:T(8,128)} custom-call(s32[1,1,2,8]{3,2,1,0:T(2,128)} %bitcast.1, s32[1,1]{1,0:T(1,128)S(6)} %copy.11.cnt, f32[2,288,288]{2,1,0:T(8,128)} %obj.1, f32[2,256,256]{2,1,0:T(8,128)} %probe.1, bf16[1,1,8,256,256]{4,3,2,1,0:T(8,128)(2,1)} %amp.1, bf16[256,256]{1,0:T(8,128)(2,1)} %constant.8.clone.table, ...), custom_call_target="tpu_custom_call" | custom-call | tf_op jit(solution)/shard_map/ptycho/pallas_call | solution.py:601
  64.4 2.1 %copy.12 = f32[2,288,288]{2,1,0:T(8,128)} copy(f32[2,288,288]{2,1,0:T(8,128)} %ptycho.1) | data formatting | bytes 1327104
